TPU v7x, 32 devices: a whole 2x2x4 slice. The times are simulated.
32 devices in a mesh: dp: 4 (over y, x), mp: 8 (over z, core).
Axes of the slice: x: 2, y: 2, z: 4, core: 2. Of those that a mesh axis runs over, the one named last changes fastest.
Arguments:
- tokens: bfloat16 [1024, 4096], P('dp'), may hold values from -96 to 96
- inner_weight: float32 [2, 4096, 16384], P(None, 'dp', 'mp'), may hold values from -5 to 5, as said below
- inner_grad: float32 [2, 4096, 16384], P(None, 'dp', 'mp'), may hold values from -400 to 400
- inner_row: float32 [2, 4096], P(None, 'dp'), may hold values from 0.01 to 1
- inner_col: float32 [2, 16384], P(None, 'mp'), may hold values from 0.01 to 1
- outer_weight: float32 [16384, 4096], P('mp', 'dp'), may hold values from -5 to 5, as said below
- outer_grad: float32 [16384, 4096], P('mp', 'dp'), may hold values from -400 to 400
- outer_row: float32 [16384], P('mp'), may hold values from 0.01 to 1
- outer_col: float32 [4096], P('dp'), may hold values from 0.01 to 1
Outputs:
- inner_new: float32 [2, 4096, 16384], P(None, 'dp', 'mp')
- inner_update: float32 [2, 4096, 16384], P(None, 'dp', 'mp')
- inner_row_new: float32 [2, 4096], P(None, 'dp')
- inner_col_new: float32 [2, 16384], P(None, 'mp')
- outer_new: float32 [16384, 4096], P('mp', 'dp')
- outer_update: float32 [16384, 4096], P('mp', 'dp')
- outer_row_new: float32 [16384], P('mp')
- outer_col_new: float32 [4096], P('dp')
- hidden: bfloat16 [1024, 16384], P('dp', 'mp')
Inputs may be any that keep to these rules, and one draw needn't show every extreme that they name: `inner_weight`: parameters of the gate and up projections. `outer_weight`: parameters of the down projection.
All inputs are finite; a program needn't handle non-finite values.
Results may differ from a plain program's by a relative error of at most 0.0058.
Values may be sent and summed in bfloat16 or wider, within the bound.
No kernel may reach another device: no remote copies, remote signals or barrier semaphores. Data moves between devices by JAX's collectives and lax.ppermute only.
A program may use at most 192 MiB of HBM per device.

v0:
```python
import functools

import jax
import jax.numpy as jnp
from jax import lax
from jax.experimental import pallas as pl
from jax.experimental.pallas import tpu as pltpu
from jax.sharding import PartitionSpec as P


D = 4096
FF = 16384
STEP = 10
FORGET = 1.0 - STEP ** (-0.8)
FRESH = 1.0 - FORGET
RELATIVE = min(0.01, STEP ** (-0.5))
LIMIT = 24 << 20


def partners(count, flip):
    return [(i, i ^ flip) for i in range(count)]


def swap(x, axis, flip):
    return lax.ppermute(x, axis, partners(lax.axis_size(axis), flip))


def total(x, axis, radix):
    count, base = lax.axis_size(axis), 1
    for width in radix:
        width = min(width, count // base)
        if width < 2:
            break
        terms = [x] + [swap(x, axis, base * k) for k in range(1, width)]
        while len(terms) > 1:
            terms = [terms[i] + terms[i + 1] for i in range(0, len(terms), 2)]
        x, base = terms[0], base * width
    assert base == count
    return x


def rounds(axis, first):
    count, out = lax.axis_size(axis), []
    left = count
    for width in (*first, *[4] * 8):
        if left > 1:
            width = min(width, left)
            out.append(width)
            left //= width
    return out


def tie(x, *after):
    return lax.optimization_barrier((x, *after))[0]


def bits_of(count):
    return [1 << i for i in range(count.bit_length() - 1)]


def far(x):
    return pltpu.with_memory_space_constraint(x, pltpu.HBM)


WHOLE = pl.BlockSpec(memory_space=pltpu.VMEM)
LEFT = pl.BlockSpec(memory_space=pl.ANY)


def tree(values):
    while len(values) > 1:
        pairs = [values[i] + values[i + 1] for i in range(0, len(values) - 1, 2)]
        values = pairs + values[len(values) - len(values) % 2 :]
    return values[0]


def fetch(source, held, sems, blocks, start=True):
    groups, depth = held.shape[:2]
    height = depth // blocks
    copies = []
    for group in range(groups):
        for block in range(blocks):
            at = (group, pl.ds(block * height, height))
            copies.append(pltpu.make_async_copy(source.at[at], held.at[at], sems.at[group * blocks + block]))
    for copy in copies if start else ():
        copy.start()
    return copies, height


def col_kernel(blocks, grad_ref, sum_ref, held, sems):
    groups, depth, columns = held.shape
    copies, height = fetch(grad_ref, held, sems, blocks)
    for group in range(groups):
        sums = jnp.zeros((8, columns), jnp.float32)
        for block in range(blocks):
            copies[group * blocks + block].wait()

            def add(i, sums):
                value = held[group, pl.ds(pl.multiple_of(block * height + i * 8, 8), 8), :]
                return sums + value * value

            sums = lax.fori_loop(0, height // 8, add, sums, unroll=4)
        sum_ref[group : group + 1, :] = jnp.sum(sums, axis=0, keepdims=True) + depth * 1e-30


def row_kernel(blocks, grad_ref, weight_ref, inverse_ref, packed_ref, held, weights, plain_ref, over_ref, sems, more):
    groups, depth, columns = held.shape
    copies, height = fetch(grad_ref, held, sems, blocks, False)
    weight_copies, _ = fetch(weight_ref, weights, more, blocks, False)
    for pair in zip(copies, weight_copies):
        for copy in pair:
            copy.start()
    ones = jnp.ones((8, 128), jnp.float32)
    across = lambda v: lax.dot_general(
        ones, v, (((1,), (1,)), ((), ())), precision=lax.Precision.HIGHEST, preferred_element_type=jnp.float32
    )
    for group in range(groups):
        inverse = jnp.broadcast_to(inverse_ref[group : group + 1, :], (8, columns))
        sums = jnp.zeros((8, columns), jnp.float32)
        for block in range(blocks):
            copies[group * blocks + block].wait()

            @pl.loop(0, height // 8, unroll=2)
            def _(i):
                at = pl.ds(pl.multiple_of(block * height + i * 8, 8), 8)
                lanes = [slice(lane, lane + 128) for lane in range(0, columns, 128)]
                squares = [held[group, at, lane] * held[group, at, lane] for lane in lanes]
                plain_ref[at, :] = tree(squares)
                over_ref[at, :] = tree([square * inverse[:, lane] for square, lane in zip(squares, lanes)])

            weight_copies[group * blocks + block].wait()

            def add(i, sums):
                value = weights[group, pl.ds(pl.multiple_of(block * height + i * 8, 8), 8), :]
                return sums + value * value

            sums = lax.fori_loop(0, height // 8, add, sums, unroll=4)
        packed_ref[group : group + 1, :depth] = across(plain_ref[...])[:1] + columns * 1e-30
        packed_ref[group : group + 1, depth : 2 * depth] = across(over_ref[...])[:1]
        packed_ref[group : group + 1, 2 * depth :] = jnp.full((1, 128), jnp.sum(sums), jnp.float32)


def statistics(kernel, bigs, small, out, more):
    big = bigs[0]
    groups, depth, _ = big.shape
    blocks = min(8, depth // 8)
    sems = pltpu.SemaphoreType.DMA((groups * blocks,))
    return pl.pallas_call(
        functools.partial(kernel, blocks),
        in_specs=[LEFT] * len(bigs) + [WHOLE] * len(small),
        out_specs=WHOLE,
        out_shape=jax.ShapeDtypeStruct(out, jnp.float32),
        scratch_shapes=[*[pltpu.VMEM(v.shape, jnp.float32) for v in bigs], *more, *[sems for _ in bigs]],
        compiler_params=pltpu.CompilerParams(vmem_limit_bytes=(6 << 20) + sum(4 * v.size for v in bigs)),
        cost_estimate=pl.CostEstimate(
            flops=4 * big.size * len(bigs), bytes_accessed=4 * big.size * len(bigs), transcendentals=0
        ),
    )(*map(far, bigs), *small)


def update_kernel(picks, coef, row_ref, col_ref, grad_ref, weight_ref, *refs):
    new_ref, update_ref, send_ref, keep_ref, cast_ref = refs[-5:]
    group = pl.program_id(0)
    width = grad_ref.shape[2]
    scale = coef[group]
    row = row_ref[0]
    for lane in range(0, width, 128):
        at = slice(lane, lane + 128)
        update = grad_ref[0, :, at] * row * (col_ref[0, :, at] * scale)
        new = weight_ref[0, :, at] + update
        update_ref[0, :, at] = update
        new_ref[0, :, at] = new
        cast_ref[:, at] = new.astype(jnp.bfloat16)
    send, keep = picks
    for ref, blocks in ((send_ref, send), (keep_ref, keep)):
        for place, block in enumerate(blocks):
            product = jnp.dot(refs[block][...], cast_ref[...], preferred_element_type=jnp.float32)
            ref[0, place] = product.astype(ref.dtype)


def update_chunk(coef, tokens, row, col, grad, weight, held, start, width, send, keep):
    groups, depth, _ = grad.shape
    count = len(send) + len(keep)
    rows = tokens[0].shape[0]
    step = min(512, width)
    first = start // step
    cols = lambda g, j: (g, 0, first + j)
    whole = pl.BlockSpec((1, depth, step), cols)
    part = lambda count: pl.BlockSpec((1, count, rows, step), lambda g, j: (g, 0, 0, j))
    out = lambda count: pltpu.HBM((groups, count, rows, width), jnp.bfloat16)
    big = jax.ShapeDtypeStruct(grad.shape, jnp.float32)
    extra = [] if held is None else list(held)
    return pl.pallas_call(
        functools.partial(update_kernel, (send, keep)),
        grid=(groups, width // step),
        in_specs=[
            pl.BlockSpec(memory_space=pltpu.SMEM),
            pl.BlockSpec((1, depth, 128), lambda g, j: (g, 0, 0)),
            pl.BlockSpec((1, 1, step), cols),
            whole,
            whole,
            *[pl.BlockSpec(piece.shape, lambda g, j: (0, 0)) for piece in tokens],
            *[LEFT for _ in extra],
        ],
        out_specs=[whole, whole, part(len(send)), part(len(keep))],
        out_shape=[big, big, out(len(send)), out(len(keep))],
        scratch_shapes=[pltpu.VMEM((depth, step), jnp.bfloat16)],
        input_output_aliases={5 + count: 0, 6 + count: 1} if extra else {},
        compiler_params=pltpu.CompilerParams(vmem_limit_bytes=LIMIT),
        cost_estimate=pl.CostEstimate(
            flops=2 * count * rows * depth * width * groups,
            bytes_accessed=groups * width * (16 * depth + 2 * count * rows),
            transcendentals=0,
        ),
        name="update_chunk",
    )(coef, row, col, far(grad), far(weight), *tokens, *extra)


def spread_kernel(factor_ref, row_ref):
    groups, depth = factor_ref.shape
    for group in range(groups):
        for start in range(0, depth, 128):
            factor = lax.rsqrt(factor_ref[group : group + 1, start : start + 128])
            row_ref[group, start : start + 128, :] = jnp.broadcast_to(factor, (128, 128)).T


def spread_rows(factor):
    shape = (*factor.shape, 128)
    return pl.pallas_call(
        spread_kernel,
        in_specs=[WHOLE],
        out_specs=WHOLE,
        out_shape=jax.ShapeDtypeStruct(shape, jnp.float32),
        compiler_params=pltpu.CompilerParams(vmem_limit_bytes=LIMIT),
        cost_estimate=pl.CostEstimate(flops=0, bytes_accessed=512 * factor.size, transcendentals=0),
        name="spread_rows",
    )(factor)


def combine_kernel(count, *refs):
    refs[-1][...] = sum(ref[...].astype(jnp.float32) for ref in refs[:count]).astype(jnp.bfloat16)


def combine(terms, blocks):
    groups, _, rows, width = terms[0][0].shape

    def pick(names):
        places = [names.index(block) for block in blocks]
        place = lambda b: functools.reduce(lambda rest, i: jnp.where(b == i, places[i], rest), range(1, len(places)), places[0])
        return pl.BlockSpec((1, 1, rows, width), lambda g, b: (g, place(b), 0, 0))

    return pl.pallas_call(
        functools.partial(combine_kernel, len(terms)),
        grid=(groups, len(blocks)),
        in_specs=[pick(names) for _, names in terms],
        out_specs=pl.BlockSpec((1, 1, rows, width), lambda g, b: (g, b, 0, 0)),
        out_shape=jax.ShapeDtypeStruct((groups, len(blocks), rows, width), jnp.bfloat16),
        compiler_params=pltpu.CompilerParams(vmem_limit_bytes=LIMIT),
        cost_estimate=pl.CostEstimate(
            flops=0, bytes_accessed=2 * (len(terms) + 1) * groups * len(blocks) * rows * width, transcendentals=0
        ),
        name="combine",
    )(*[value for value, _ in terms])


def final_kernel(counts, *refs):
    out_ref, place, start = refs[-1], 0, 0
    for count in counts:
        terms = refs[place : place + count]
        gate, up = [sum(ref[g, 0].astype(jnp.float32) for ref in terms) for g in range(2)]
        width = gate.shape[1]
        out_ref[:, start : start + width] = (jax.nn.gelu(gate, approximate=True) * up).astype(out_ref.dtype)
        place, start = place + count, start + width


def finish(chunks):
    rows = chunks[0][0][0].shape[2]
    columns = sum(terms[0][0].shape[3] for terms in chunks)
    height = rows // 4
    terms = [term for chunk in chunks for term in chunk]
    spec = lambda value, place: pl.BlockSpec((2, 1, height, value.shape[3]), lambda i: (0, place, i, 0))
    return pl.pallas_call(
        functools.partial(final_kernel, [len(chunk) for chunk in chunks]),
        grid=(rows // height,),
        in_specs=[spec(value, place) for value, place in terms],
        out_specs=pl.BlockSpec((height, columns), lambda i: (i, 0)),
        out_shape=jax.ShapeDtypeStruct((rows, columns), jnp.bfloat16),
        compiler_params=pltpu.CompilerParams(vmem_limit_bytes=LIMIT),
        cost_estimate=pl.CostEstimate(
            flops=0, bytes_accessed=20 * rows * columns, transcendentals=rows * columns
        ),
        name="finish",
    )(*[value for value, _ in terms])


def plan(columns, count):
    bits = bits_of(count)
    pieces = min(4, columns // 128)
    width = columns // pieces
    return [
        (i * width, width, bits[i % len(bits) :] + bits[: i % len(bits)]) for i in range(pieces)
    ]


def split(blocks, bit):
    return [b for b in blocks if b & bit], [b for b in blocks if not b & bit]


def program(
    tokens, inner_weight, inner_grad, inner_row, inner_col, outer_weight, outer_grad, outer_row, outer_col
):
    data_count = lax.axis_size("dp")
    data_index = lax.axis_index("dp")
    groups, depth, columns = inner_grad.shape
    sum_data = lambda v: total(v, "dp", rounds("dp", (4,)))
    sum_model = lambda v: total(v, "mp", rounds("mp", (2,)))

    col_part = statistics(col_kernel, (inner_grad,), (), (groups, columns), ())
    col_sum = sum_data(col_part)
    inner_col_new = FORGET * inner_col + FRESH * (col_sum / D)
    inverse_col = 1.0 / inner_col_new
    tokens_late = tie(tokens, col_part)
    share = []
    for flip in range(data_count):
        piece = lax.dynamic_slice_in_dim(tokens_late, (data_index ^ flip) * depth, depth, 1)
        share.append(piece if flip == 0 else swap(piece, "dp", flip))

    columned = [pltpu.VMEM((depth, 128), jnp.float32)] * 2
    packed = statistics(row_kernel, (inner_grad, inner_weight), (inverse_col,), (groups, 2 * depth + 128), columned)
    outer_grad = tie(outer_grad, packed)
    outer_sq = outer_grad * outer_grad
    outer_part = jnp.sum(outer_sq + 1e-30, axis=1)
    outer_weight = tie(outer_weight, packed)
    outer_weight_sq = jnp.sum(outer_weight * outer_weight)
    packed = sum_model(packed)
    row_sum, weighted, weight_sq = packed[:, :depth], packed[:, depth : 2 * depth], packed[:, 2 * depth]
    inner_row_new = FORGET * inner_row + FRESH * (row_sum / FF)
    scalars = jnp.stack([jnp.sum(inner_row_new, 1), jnp.sum(weighted / inner_row_new, 1), weight_sq], 1)
    scalars = jnp.broadcast_to(scalars[:, :, None], (groups, 3, 128)).reshape(-1)
    scalars = sum_data(jnp.concatenate([outer_part, scalars]))
    outer_row_sum = scalars[: outer_part.size]
    scalars = scalars[outer_part.size :].reshape(groups, 3, 128)[:, :, 0]
    mean = scalars[:, 0] / D
    clip = jnp.maximum(1.0, jnp.sqrt(mean * scalars[:, 1] / (D * FF)))
    step = RELATIVE * jnp.sqrt(scalars[:, 2] / (D * FF))
    coef = -(step / clip) * jnp.sqrt(mean)
    row = spread_rows(inner_row_new)
    col = lax.rsqrt(inner_col_new)[:, None, :]

    held, chunks = None, []
    for start, width, order in plan(columns, data_count):
        send, keep = split(list(range(data_count)), order[0])
        *held, sent, kept = update_chunk(
            coef, share, row, col, inner_grad, inner_weight, held, start, width, send, keep
        )
        came = swap(sent, "dp", order[0])
        chunks.append((start, width, order, keep, [(kept, keep), (came, keep)]))
    inner_new, inner_update = held

    for level in range(1, len(bits_of(data_count))):
        later = []
        for start, width, order, blocks, terms in chunks:
            send, keep = split(blocks, order[level])
            sent = combine(terms, send)
            came = swap(sent, "dp", order[level])
            later.append((start, width, order, keep, [*terms, (came, keep)]))
        chunks = later
    hidden = finish([[(value, names.index(0)) for value, names in terms] for *_, terms in chunks])

    outer_row_new = FORGET * outer_row + FRESH * (outer_row_sum / D)
    outer_grad = tie(outer_grad, outer_row_new)
    outer_sq = outer_grad * outer_grad
    col_sum = jnp.sum(outer_sq + 1e-30, axis=0)
    weighted = jnp.sum(outer_sq * (1.0 / outer_row_new)[:, None], axis=0)
    spare = jnp.broadcast_to(jnp.stack([outer_weight_sq, jnp.sum(outer_row_new)])[:, None], (2, 128)).reshape(-1)
    packed = jnp.concatenate([col_sum, weighted, spare])
    packed = sum_model(packed)
    width = outer_col.shape[0]
    outer_col_new = FORGET * outer_col + FRESH * (packed[:width] / FF)
    scalars = jnp.stack([jnp.sum(packed[width : 2 * width] / outer_col_new), packed[2 * width]])
    scalars = sum_data(jnp.broadcast_to(scalars[:, None], (2, 128)))[:, 0]
    mean = packed[2 * width + 128] / FF
    clip = jnp.maximum(1.0, jnp.sqrt(mean * scalars[0] / (D * FF)))
    step = RELATIVE * jnp.sqrt(scalars[1] / (D * FF))
    scale = -(step / clip) * jnp.sqrt(mean)
    outer_update = outer_grad * (lax.rsqrt(outer_row_new)[:, None] * (lax.rsqrt(outer_col_new) * scale)[None, :])
    outer_new = outer_weight + outer_update
    return (
        inner_new,
        inner_update,
        inner_row_new,
        inner_col_new,
        outer_new,
        outer_update,
        outer_row_new,
        outer_col_new,
        hidden,
    )


def solution(mesh):
    placed = (
        P("dp", None),
        P(None, "dp", "mp"),
        P(None, "dp", "mp"),
        P(None, "dp"),
        P(None, "mp"),
        P("mp", "dp"),
        P("mp", "dp"),
        P("mp"),
        P("dp"),
    )
    return jax.shard_map(
        program,
        mesh=mesh,
        in_specs=placed,
        out_specs=(
            P(None, "dp", "mp"),
            P(None, "dp", "mp"),
            P(None, "dp"),
            P(None, "mp"),
            P("mp", "dp"),
            P("mp", "dp"),
            P("mp"),
            P("dp"),
            P("dp", "mp"),
        ),
        check_vma=False,
    )
```

profile of v0, /device:TPU:0, one launch (start us, length us, event | category | flops | bytes accessed | tf_op | source)
XLA Modules:
  0.0 178.3 jit_solution(8772796024323188978)
XLA Ops:
  0.7 6.1 %shard_map.160 = f32[2,2048]{1,0:T(2,128)S(1)} custom-call(f32[2,1024,2048]{2,1,0:T(8,128)} %grad_ref.11), custom_call_target="tpu_custom_call" | custom-call | flops 16777216 | bytes 16777216 | tf_op jit(solution)/shard_map/pallas_call | solution.py:147
  6.7 3.0 %collective-permute-start = (f32[2,2048]{1,0:T(2,128)S(1)}, f32[2,2048]{1,0:T(2,128)S(1)}, u32[]{:S(2)}, u32[]{:S(2)}) collective-permute-start(f32[2,2048]{1,0:T(2,128)S(1)} %shard_map.160), channel_id=1, source_target_pairs={{0,8},{8,0},{16,24},{24,16},{1,9},{9,1},{17,25},{25,17},{2,10},{10... | collective-permute-start | bytes 49160 | tf_op jit(solution)/shard_map/ppermute | solution.py:25
  9.7 1.5 collective-permute-start.1
  11.3 0.2 collective-permute-done
  11.5 2.0 %collective-permute-done.1 = f32[2,2048]{1,0:T(2,128)S(1)} collective-permute-done((f32[2,2048]{1,0:T(2,128)S(1)}, f32[2,2048]{1,0:T(2,128)S(1)}, u32[]{:S(2)}, u32[]{:S(2)}) %collective-permute-start.1) | collective-permute-done | bytes 16416 | tf_op jit(solution)/shard_map/ppermute | solution.py:25
  13.5 2.4 %collective-permute-done.2 = f32[2,2048]{1,0:T(2,128)S(1)} collective-permute-done((f32[2,2048]{1,0:T(2,128)S(1)}, f32[2,2048]{1,0:T(2,128)S(1)}, u32[]{:S(2)}, u32[]{:S(2)}) %collective-permute-start.2) | collective-permute-done | bytes 16416 | tf_op jit(solution)/shard_map/ppermute | solution.py:25
  16.0 12.0 %shard_map.161 = f32[2,2176]{1,0:T(2,128)S(1)} custom-call(f32[2,1024,2048]{2,1,0:T(8,128)} %grad_ref.11, f32[2,1024,2048]{2,1,0:T(8,128)} %weight_ref.9, f32[2,2048]{1,0:T(2,128)S(1)} %broadcast_divide_fusion.inverse_ref), custom_call_target="tpu_custom_call" | custom-call | flops 33554432 | bytes 33554432 | tf_op jit(solution)/shard_map/pallas_call | solution.py:147
  28.1 1.2 constant_dynamic-slice_fusion
  29.3 0.5 collective-permute-start.10
  29.9 2.1 %collective-permute-start.4 = (f32[2,2176]{1,0:T(2,128)S(1)}, f32[2,2176]{1,0:T(2,128)S(1)}, u32[]{:S(2)}, u32[]{:S(2)}) collective-permute-start(f32[2,2176]{1,0:T(2,128)S(1)} %add.89), channel_id=1, source_target_pairs={{0,2},{1,3},{2,0},{3,1},{4,6},{5,7},{6,4},{7,5},{8,10},{9,11},{10,... | collective-permute-start | bytes 52232 | tf_op jit(solution)/shard_map/ppermute | solution.py:25
  32.0 2.6 %collective-permute-start.5 = (f32[2,2176]{1,0:T(2,128)S(1)}, f32[2,2176]{1,0:T(2,128)S(1)}, u32[]{:S(2)}, u32[]{:S(2)}) collective-permute-start(f32[2,2176]{1,0:T(2,128)S(1)} %add.89), channel_id=1, source_target_pairs={{0,4},{1,5},{2,6},{3,7},{4,0},{5,1},{6,2},{7,3},{8,12},{9,13},{10,... | collective-permute-start | bytes 52232 | tf_op jit(solution)/shard_map/ppermute | solution.py:25
  34.6 0.9 add_reduce_fusion.1
  35.5 1.3 collective-permute-done.5
  36.8 3.3 %collective-permute-done.6 = f32[2,2176]{1,0:T(2,128)S(1)} collective-permute-done((f32[2,2176]{1,0:T(2,128)S(1)}, f32[2,2176]{1,0:T(2,128)S(1)}, u32[]{:S(2)}, u32[]{:S(2)}) %collective-permute-start.6) | collective-permute-done | bytes 17440 | tf_op jit(solution)/shard_map/ppermute | solution.py:25
  40.2 0.2 fusion.6
  40.4 0.1 copy.28
  40.5 0.1 copy.29
  40.6 0.1 pad_maximum_fusion.2
  40.7 1.5 collective-permute-start.7
  42.3 1.5 collective-permute-start.8
  43.8 0.5 collective-permute-start.9
  44.3 6.1 %multiply_reduce_fusion = f32[]{:T(128)} fusion(f32[2048,1024]{1,0:T(8,128)} %param.14), kind=kLoop, calls=%fused_computation.1 | loop fusion | flops 4194303 | bytes 8388612 | tf_op jit(solution)/shard_map/reduce_sum | solution.py:333
  50.4 0.3 spread_rows.1.row_ref
  50.8 2.5 %collective-permute-start.12 = (bf16[256,1024]{1,0:T(8,128)(2,1)}, bf16[256,1024]{1,0:T(8,128)(2,1)S(1)}, u32[]{:S(2)}, u32[]{:S(2)}) collective-permute-start(bf16[256,1024]{1,0:T(8,128)(2,1)} %get-tuple-element.62), channel_id=1, source_target_pairs={{0,24},{8,16},{16,8},{24,0},{1,25},{9,17},{17,9},{25,1},{2,26},{10... | collective-permute-start | bytes 1572872 | tf_op jit(solution)/shard_map/ppermute | solution.py:25
  53.4 0.6 broadcast_divide_fusion.1
  54.0 1.4 pad_maximum_fusion.3
  55.4 4.2 %add_reduce_fusion = (f32[1024]{0:T(1024)S(1)}, f32[1024]{0:T(1024)S(1)}) fusion(f32[2048,1024]{1,0:T(8,128)} %param.15, f32[2048]{0:T(1024)S(1)} %get-tuple-element.68), kind=kLoop, calls=%fused_computation.3 | loop fusion | flops 10483712 | bytes 8404992 | tf_op jit(solution)/shard_map/reduce_sum | solution.py:372
  59.7 0.1 slice_reduce_fusion
  59.8 0.2 multiply_reduce_fusion.2.coef
  60.0 0.9 collective-permute-done.13
  60.9 0.8 collective-permute-start.15
  61.7 3.6 %collective-permute-start.16 = (f32[2304]{0:T(1024)S(1)}, f32[2304]{0:T(1024)S(1)}, u32[]{:S(2)}, u32[]{:S(2)}) collective-permute-start(f32[2304]{0:T(1024)S(1)} %fusion.5), channel_id=1, source_target_pairs={{0,6},{1,7},{2,4},{3,5},{4,2},{5,3},{6,0},{7,1},{8,14},{9,15},{10,... | collective-permute-start | bytes 27656 | tf_op jit(solution)/shard_map/ppermute | solution.py:25
  65.3 6.8 %update_chunk.4 = (f32[2,1024,2048]{2,1,0:T(8,128)}, f32[2,1024,2048]{2,1,0:T(8,128)}, bf16[2,2,256,512]{3,2,1,0:T(8,128)(2,1)}, bf16[2,2,256,512]{3,2,1,0:T(8,128)(2,1)}) custom-call(f32[2]{0:T(128)S(1)} %multiply_reduce_fusion.2.coef, f32[2,1024,128]{2,1,0:T(8,128)S(1)} %spread_rows.1.row_ref, f32[2,1,2048]{2,1,0:T(1,128)S(1)} %broadcast_in_dim.9.col_ref, ...), custom_call_target="tpu_custom_call" | custom-call | flops 2147483648 | bytes 18874368 | tf_op jit(solution)/shard_map/update_chunk/pallas_call | solution.py:192
  72.0 6.8 %update_chunk.5 = (f32[2,1024,2048]{2,1,0:T(8,128)}, f32[2,1024,2048]{2,1,0:T(8,128)}, bf16[2,2,256,512]{3,2,1,0:T(8,128)(2,1)}, bf16[2,2,256,512]{3,2,1,0:T(8,128)(2,1)}) custom-call(f32[2]{0:T(128)S(1)} %multiply_reduce_fusion.2.coef, f32[2,1024,128]{2,1,0:T(8,128)S(1)} %spread_rows.1.row_ref, ...), custom_call_target="tpu_custom_call", output_to_operand_aliasing={{0}: (9, {}), {1}: (10, {})} | custom-call | flops 2147483648 | bytes 18874368 | tf_op jit(solution)/shard_map/update_chunk/pallas_call | solution.py:192
  78.8 6.8 %update_chunk.6 = (f32[2,1024,2048]{2,1,0:T(8,128)}, f32[2,1024,2048]{2,1,0:T(8,128)}, bf16[2,2,256,512]{3,2,1,0:T(8,128)(2,1)}, bf16[2,2,256,512]{3,2,1,0:T(8,128)(2,1)}) custom-call(f32[2]{0:T(128)S(1)} %multiply_reduce_fusion.2.coef, f32[2,1024,128]{2,1,0:T(8,128)S(1)} %spread_rows.1.row_ref, ...), custom_call_target="tpu_custom_call", output_to_operand_aliasing={{0}: (9, {}), {1}: (10, {})} | custom-call | flops 2147483648 | bytes 18874368 | tf_op jit(solution)/shard_map/update_chunk/pallas_call | solution.py:192
  85.6 6.9 %update_chunk.7 = (f32[2,1024,2048]{2,1,0:T(8,128)}, f32[2,1024,2048]{2,1,0:T(8,128)}, bf16[2,2,256,512]{3,2,1,0:T(8,128)(2,1)}, bf16[2,2,256,512]{3,2,1,0:T(8,128)(2,1)}) custom-call(f32[2]{0:T(128)S(1)} %multiply_reduce_fusion.2.coef, f32[2,1024,128]{2,1,0:T(8,128)S(1)} %spread_rows.1.row_ref, ...), custom_call_target="tpu_custom_call", output_to_operand_aliasing={{0}: (9, {}), {1}: (10, {})} | custom-call | flops 2147483648 | bytes 18874368 | tf_op jit(solution)/shard_map/update_chunk/pallas_call | solution.py:192
  92.5 0.5 collective-permute-start.26
  93.0 0.5 collective-permute-start.24
  93.6 1.5 collective-permute-start.22
  95.1 1.5 collective-permute-start.20
  96.6 0.5 fusion.13
  97.1 0.7 fusion.4
  97.8 1.3 pad_maximum_fusion.4
  99.2 0.5 collective-permute-start.17
  99.8 40.2 %collective-permute-done.17 = f32[2,128]{1,0:T(2,128)S(1)} collective-permute-done((f32[2,128]{1,0:T(2,128)S(1)}, f32[2,128]{1,0:T(2,128)S(1)}, u32[]{:S(2)}, u32[]{:S(2)}) %collective-permute-start.17) | collective-permute-done | bytes 1056 | tf_op jit(solution)/shard_map/ppermute | solution.py:25
  139.9 1.5 collective-permute-start.18
  141.5 2.1 %collective-permute-done.18 = f32[2,128]{1,0:T(2,128)S(1)} collective-permute-done((f32[2,128]{1,0:T(2,128)S(1)}, f32[2,128]{1,0:T(2,128)S(1)}, u32[]{:S(2)}, u32[]{:S(2)}) %collective-permute-start.18) | collective-permute-done | bytes 1056 | tf_op jit(solution)/shard_map/ppermute | solution.py:25
  143.5 1.5 collective-permute-start.19
  145.7 2.3 %collective-permute-done.19 = f32[2,128]{1,0:T(2,128)S(1)} collective-permute-done((f32[2,128]{1,0:T(2,128)S(1)}, f32[2,128]{1,0:T(2,128)S(1)}, u32[]{:S(2)}, u32[]{:S(2)}) %collective-permute-start.19) | collective-permute-done | bytes 1056 | tf_op jit(solution)/shard_map/ppermute | solution.py:25
  148.1 0.6 fusion.14
  150.0 1.2 copy-done.5
  151.2 0.1 combine.7
  151.4 0.6 collective-permute-start.27
  152.0 1.2 copy-done.3
  153.2 0.1 combine.6
  153.4 1.6 collective-permute-start.25
  155.0 1.2 copy-done.1
  156.2 1.1 combine.5
  157.3 1.6 collective-permute-start.23
  158.9 1.1 combine.4
  160.0 0.6 collective-permute-start.21
  160.6 11.9 %fusion.7 = (f32[2048,1024]{1,0:T(8,128)}, f32[2048,1024]{1,0:T(8,128)}) fusion(f32[2048,1024]{1,0:T(8,128)} %param.14, f32[2048,1024]{1,0:T(8,128)} %param.15, f32[1024]{0:T(1024)S(1)} %rsqrt_multiply_fusion, f32[2048]{0:T(1024)S(1)} %get-tuple-element.55), kind=kLoop, calls=%fused_computation.38 | loop fusion | flops 6291456 | bytes 33566720 | tf_op jit(solution)/shard_map/add | solution.py:386
  172.5 1.7 collective-permute-done.21.refs_2_
  174.1 4.1 %finish.1 = bf16[256,2048]{1,0:T(8,128)(2,1)} custom-call(bf16[2,2,256,512]{3,2,1,0:T(8,128)(2,1)S(1)} %copy-done, bf16[2,2,256,512]{3,2,1,0:T(8,128)(2,1)} %collective-permute-done.20.refs_1_, bf16[2,1,256,512]{3,2,1,0:T(8,128)(2,1)S(1)} %collective-permute-done.21.refs_2_, bf16[2,2,256,512]{3,2,1,0:T(8,128)(2,1)S(1)} %copy-done.2, ...), custom_call_target="tpu_custom_call" | custom-call | bytes 10485760 | tf_op jit(solution)/shard_map/finish/pallas_call | solution.py:281
  (75 shorter events, 0.8 us)
Async XLA Ops:
  0.6 15.3 %copy-start.12 = (f32[2,2048]{1,0:T(2,128)S(1)}, f32[2,2048]{1,0:T(2,128)}, u32[]{:S(2)}) copy-start(f32[2,2048]{1,0:T(2,128)} %param.13) | copy-start | bytes 49156
  6.7 4.8 %collective-permute-start = (f32[2,2048]{1,0:T(2,128)S(1)}, f32[2,2048]{1,0:T(2,128)S(1)}, u32[]{:S(2)}, u32[]{:S(2)}) collective-permute-start(f32[2,2048]{1,0:T(2,128)S(1)} %shard_map.160), channel_id=1, source_target_pairs={{0,8},{8,0},{16,24},{24,16},{1,9},{9,1},{17,25},{25,17},{2,10},{10... | collective-permute-start | bytes 49160 | tf_op jit(solution)/shard_map/ppermute | solution.py:25
  9.7 3.7 %collective-permute-start.1 = (f32[2,2048]{1,0:T(2,128)S(1)}, f32[2,2048]{1,0:T(2,128)S(1)}, u32[]{:S(2)}, u32[]{:S(2)}) collective-permute-start(f32[2,2048]{1,0:T(2,128)S(1)} %shard_map.160), channel_id=1, source_target_pairs={{0,16},{8,24},{16,0},{24,8},{1,17},{9,25},{17,1},{25,9},{2,18},{10... | collective-permute-start | bytes 49160 | tf_op jit(solution)/shard_map/ppermute | solution.py:25
  11.3 4.6 %collective-permute-start.2 = (f32[2,2048]{1,0:T(2,128)S(1)}, f32[2,2048]{1,0:T(2,128)S(1)}, u32[]{:S(2)}, u32[]{:S(2)}) collective-permute-start(f32[2,2048]{1,0:T(2,128)S(1)} %shard_map.160), channel_id=1, source_target_pairs={{0,24},{8,16},{16,8},{24,0},{1,25},{9,17},{17,9},{25,1},{2,26},{10... | collective-permute-start | bytes 49160 | tf_op jit(solution)/shard_map/ppermute | solution.py:25
  15.9 12.1 %copy-start.10 = (f32[2,2048]{1,0:T(2,128)}, f32[2,2048]{1,0:T(2,128)S(1)}, u32[]{:S(2)}) copy-start(f32[2,2048]{1,0:T(2,128)S(1)} %get-tuple-element.60) | copy-start | bytes 49156
  16.0 12.1 %copy-start.9 = (bf16[256,4096]{1,0:T(8,128)(2,1)S(1)}, bf16[256,4096]{1,0:T(8,128)(2,1)}, u32[]{:S(2)}) copy-start(bf16[256,4096]{1,0:T(8,128)(2,1)} %param.9) | copy-start | bytes 6291460
  16.0 18.6 %copy-start.8 = (f32[2048,1024]{1,0:T(8,128)S(1)}, f32[2048,1024]{1,0:T(8,128)}, u32[]{:S(2)}) copy-start(f32[2048,1024]{1,0:T(8,128)} %param.15) | copy-start | bytes 25165828
  28.0 12.2 %copy-start.14 = (f32[2,1024]{1,0:T(2,128)S(1)}, f32[2,1024]{1,0:T(2,128)}, u32[]{:S(2)}) copy-start(f32[2,1024]{1,0:T(2,128)} %param.12) | copy-start | bytes 24580
  28.0 1.9 %collective-permute-start.3 = (f32[2,2176]{1,0:T(2,128)S(1)}, f32[2,2176]{1,0:T(2,128)S(1)}, u32[]{:S(2)}, u32[]{:S(2)}) collective-permute-start(f32[2,2176]{1,0:T(2,128)S(1)} %shard_map.161), channel_id=1, source_target_pairs={{0,1},{1,0},{2,3},{3,2},{4,5},{5,4},{6,7},{7,6},{8,9},{9,8},{10,11... | collective-permute-start | bytes 52232 | tf_op jit(solution)/shard_map/ppermute | solution.py:25
  29.3 32.3 %collective-permute-start.10 = (bf16[256,1024]{1,0:T(8,128)(2,1)}, bf16[256,1024]{1,0:T(8,128)(2,1)S(1)}, u32[]{:S(2)}, u32[]{:S(2)}) collective-permute-start(bf16[256,1024]{1,0:T(8,128)(2,1)} %get-tuple-element.64), channel_id=1, source_target_pairs={{0,8},{8,0},{16,24},{24,16},{1,9},{9,1},{17,25},{25,17},{2,10},{10... | collective-permute-start | bytes 1572872 | tf_op jit(solution)/shard_map/ppermute | solution.py:25
  29.9 35.4 %collective-permute-start.11 = (bf16[256,1024]{1,0:T(8,128)(2,1)}, bf16[256,1024]{1,0:T(8,128)(2,1)S(1)}, u32[]{:S(2)}, u32[]{:S(2)}) collective-permute-start(bf16[256,1024]{1,0:T(8,128)(2,1)} %get-tuple-element.63), channel_id=1, source_target_pairs={{0,16},{8,24},{16,0},{24,8},{1,17},{9,25},{17,1},{25,9},{2,18},{10... | collective-permute-start | bytes 1572872 | tf_op jit(solution)/shard_map/ppermute | solution.py:25
  29.9 23.4 %copy-start.15 = (f32[2048]{0:T(1024)S(1)}, f32[2048]{0:T(1024)}, u32[]{:S(2)}) copy-start(f32[2048]{0:T(1024)} %param.16) | copy-start | bytes 24580
  29.9 5.6 %collective-permute-start.4 = (f32[2,2176]{1,0:T(2,128)S(1)}, f32[2,2176]{1,0:T(2,128)S(1)}, u32[]{:S(2)}, u32[]{:S(2)}) collective-permute-start(f32[2,2176]{1,0:T(2,128)S(1)} %add.89), channel_id=1, source_target_pairs={{0,2},{1,3},{2,0},{3,1},{4,6},{5,7},{6,4},{7,5},{8,10},{9,11},{10,... | collective-permute-start | bytes 52232 | tf_op jit(solution)/shard_map/ppermute | solution.py:25
  32.0 4.8 %collective-permute-start.5 = (f32[2,2176]{1,0:T(2,128)S(1)}, f32[2,2176]{1,0:T(2,128)S(1)}, u32[]{:S(2)}, u32[]{:S(2)}) collective-permute-start(f32[2,2176]{1,0:T(2,128)S(1)} %add.89), channel_id=1, source_target_pairs={{0,4},{1,5},{2,6},{3,7},{4,0},{5,1},{6,2},{7,3},{8,12},{9,13},{10,... | collective-permute-start | bytes 52232 | tf_op jit(solution)/shard_map/ppermute | solution.py:25
  34.6 5.5 %collective-permute-start.6 = (f32[2,2176]{1,0:T(2,128)S(1)}, f32[2,2176]{1,0:T(2,128)S(1)}, u32[]{:S(2)}, u32[]{:S(2)}) collective-permute-start(f32[2,2176]{1,0:T(2,128)S(1)} %add.89), channel_id=1, source_target_pairs={{0,6},{1,7},{2,4},{3,5},{4,2},{5,3},{6,0},{7,1},{8,14},{9,15},{10,... | collective-permute-start | bytes 52232 | tf_op jit(solution)/shard_map/ppermute | solution.py:25
  40.4 19.2 %copy-start.7 = (f32[2,1024]{1,0:T(2,128)}, f32[2,1024]{1,0:T(2,128)S(1)}, u32[]{:S(2)}) copy-start(f32[2,1024]{1,0:T(2,128)S(1)} %get-tuple-element.61.factor_ref) | copy-start | bytes 24580
  40.7 10.0 %collective-permute-start.7 = (f32[2816]{0:T(1024)S(1)}, f32[2816]{0:T(1024)S(1)}, u32[]{:S(2)}, u32[]{:S(2)}) collective-permute-start(f32[2816]{0:T(1024)S(1)} %pad_maximum_fusion), channel_id=1, source_target_pairs={{0,8},{8,0},{16,24},{24,16},{1,9},{9,1},{17,25},{25,17},{2,10},{10... | collective-permute-start | bytes 33800 | tf_op jit(solution)/shard_map/ppermute | solution.py:25
  42.3 11.0 %collective-permute-start.8 = (f32[2816]{0:T(1024)S(1)}, f32[2816]{0:T(1024)S(1)}, u32[]{:S(2)}, u32[]{:S(2)}) collective-permute-start(f32[2816]{0:T(1024)S(1)} %pad_maximum_fusion), channel_id=1, source_target_pairs={{0,16},{8,24},{16,0},{24,8},{1,17},{9,25},{17,1},{25,9},{2,18},{10... | collective-permute-start | bytes 33800 | tf_op jit(solution)/shard_map/ppermute | solution.py:25
  43.8 9.5 %collective-permute-start.9 = (f32[2816]{0:T(1024)S(1)}, f32[2816]{0:T(1024)S(1)}, u32[]{:S(2)}, u32[]{:S(2)}) collective-permute-start(f32[2816]{0:T(1024)S(1)} %pad_maximum_fusion), channel_id=1, source_target_pairs={{0,24},{8,16},{16,8},{24,0},{1,25},{9,17},{17,9},{25,1},{2,26},{10... | collective-permute-start | bytes 33800 | tf_op jit(solution)/shard_map/ppermute | solution.py:25
  50.8 14.5 %collective-permute-start.12 = (bf16[256,1024]{1,0:T(8,128)(2,1)}, bf16[256,1024]{1,0:T(8,128)(2,1)S(1)}, u32[]{:S(2)}, u32[]{:S(2)}) collective-permute-start(bf16[256,1024]{1,0:T(8,128)(2,1)} %get-tuple-element.62), channel_id=1, source_target_pairs={{0,24},{8,16},{16,8},{24,0},{1,25},{9,17},{17,9},{25,1},{2,26},{10... | collective-permute-start | bytes 1572872 | tf_op jit(solution)/shard_map/ppermute | solution.py:25
  53.4 18.7 %copy-start.11 = (f32[2048]{0:T(1024)}, f32[2048]{0:T(1024)S(1)}, u32[]{:S(2)}) copy-start(f32[2048]{0:T(1024)S(1)} %get-tuple-element.56) | copy-start | bytes 24580
  59.6 1.2 collective-permute-start.13
  60.9 32.7 %collective-permute-start.14 = (f32[2304]{0:T(1024)S(1)}, f32[2304]{0:T(1024)S(1)}, u32[]{:S(2)}, u32[]{:S(2)}) collective-permute-start(f32[2304]{0:T(1024)S(1)} %fusion.5), channel_id=1, source_target_pairs={{0,2},{1,3},{2,0},{3,1},{4,6},{5,7},{6,4},{7,5},{8,10},{9,11},{10,... | collective-permute-start | bytes 27656 | tf_op jit(solution)/shard_map/ppermute | solution.py:25
  60.9 34.2 %collective-permute-start.15 = (f32[2304]{0:T(1024)S(1)}, f32[2304]{0:T(1024)S(1)}, u32[]{:S(2)}, u32[]{:S(2)}) collective-permute-start(f32[2304]{0:T(1024)S(1)} %fusion.5), channel_id=1, source_target_pairs={{0,4},{1,5},{2,6},{3,7},{4,0},{5,1},{6,2},{7,3},{8,12},{9,13},{10,... | collective-permute-start | bytes 27656 | tf_op jit(solution)/shard_map/ppermute | solution.py:25
  61.7 34.9 %collective-permute-start.16 = (f32[2304]{0:T(1024)S(1)}, f32[2304]{0:T(1024)S(1)}, u32[]{:S(2)}, u32[]{:S(2)}) collective-permute-start(f32[2304]{0:T(1024)S(1)} %fusion.5), channel_id=1, source_target_pairs={{0,6},{1,7},{2,4},{3,5},{4,2},{5,3},{6,0},{7,1},{8,14},{9,15},{10,... | collective-permute-start | bytes 27656 | tf_op jit(solution)/shard_map/ppermute | solution.py:25
  85.6 11.6 %copy-start.16 = (f32[1024]{0:T(1024)S(1)}, f32[1024]{0:T(1024)}, u32[]{:S(2)}) copy-start(f32[1024]{0:T(1024)} %param.17) | copy-start | bytes 12292
  92.5 66.4 %copy-start = (bf16[2,2,256,512]{3,2,1,0:T(8,128)(2,1)S(1)}, bf16[2,2,256,512]{3,2,1,0:T(8,128)(2,1)}, u32[]{:S(2)}) copy-start(bf16[2,2,256,512]{3,2,1,0:T(8,128)(2,1)} %get-tuple-element.41.refs_0_) | copy-start | bytes 3145732
  92.5 57.5 %collective-permute-start.26 = (bf16[2,2,256,512]{3,2,1,0:T(8,128)(2,1)}, bf16[2,2,256,512]{3,2,1,0:T(8,128)(2,1)S(1)}, u32[]{:S(2)}, u32[]{:S(2)}) collective-permute-start(bf16[2,2,256,512]{3,2,1,0:T(8,128)(2,1)} %get-tuple-element.48), channel_id=1, source_target_pairs={{0,16},{8,24},{16,0},{24,8},{1,17},{9,25},{17,1},{25,9},{2,18},{10... | collective-permute-start | bytes 3145736 | tf_op jit(solution)/shard_map/ppermute | solution.py:25
  93.0 59.0 %collective-permute-start.24 = (bf16[2,2,256,512]{3,2,1,0:T(8,128)(2,1)}, bf16[2,2,256,512]{3,2,1,0:T(8,128)(2,1)S(1)}, u32[]{:S(2)}, u32[]{:S(2)}) collective-permute-start(bf16[2,2,256,512]{3,2,1,0:T(8,128)(2,1)} %get-tuple-element.46), channel_id=1, source_target_pairs={{0,8},{8,0},{16,24},{24,16},{1,9},{9,1},{17,25},{25,17},{2,10},{10... | collective-permute-start | bytes 3145736 | tf_op jit(solution)/shard_map/ppermute | solution.py:25
  93.6 61.4 %collective-permute-start.22 = (bf16[2,2,256,512]{3,2,1,0:T(8,128)(2,1)}, bf16[2,2,256,512]{3,2,1,0:T(8,128)(2,1)}, u32[]{:S(2)}, u32[]{:S(2)}) collective-permute-start(bf16[2,2,256,512]{3,2,1,0:T(8,128)(2,1)} %get-tuple-element.44), channel_id=1, source_target_pairs={{0,16},{8,24},{16,0},{24,8},{1,17},{9,25},{17,1},{25,9},{2,18},{10... | collective-permute-start | bytes 3145736 | tf_op jit(solution)/shard_map/ppermute | solution.py:25
  95.1 63.8 %collective-permute-start.20 = (bf16[2,2,256,512]{3,2,1,0:T(8,128)(2,1)}, bf16[2,2,256,512]{3,2,1,0:T(8,128)(2,1)}, u32[]{:S(2)}, u32[]{:S(2)}) collective-permute-start(bf16[2,2,256,512]{3,2,1,0:T(8,128)(2,1)} %get-tuple-element.42), channel_id=1, source_target_pairs={{0,8},{8,0},{16,24},{24,16},{1,9},{9,1},{17,25},{25,17},{2,10},{10... | collective-permute-start | bytes 3145736 | tf_op jit(solution)/shard_map/ppermute | solution.py:25
  97.8 74.6 %copy-start.13 = (f32[1024]{0:T(1024)}, f32[1024]{0:T(1024)S(1)}, u32[]{:S(2)}) copy-start(f32[1024]{0:T(1024)S(1)} %get-tuple-element.58) | copy-start | bytes 12292
  99.2 40.7 %collective-permute-start.17 = (f32[2,128]{1,0:T(2,128)S(1)}, f32[2,128]{1,0:T(2,128)S(1)}, u32[]{:S(2)}, u32[]{:S(2)}) collective-permute-start(f32[2,128]{1,0:T(2,128)S(1)} %broadcast_in_dim.11), channel_id=1, source_target_pairs={{0,8},{8,0},{16,24},{24,16},{1,9},{9,1},{17,25},{25,17},{2,10},{10... | collective-permute-start | bytes 3080 | tf_op jit(solution)/shard_map/ppermute | solution.py:25
  139.9 3.6 %collective-permute-start.18 = (f32[2,128]{1,0:T(2,128)S(1)}, f32[2,128]{1,0:T(2,128)S(1)}, u32[]{:S(2)}, u32[]{:S(2)}) collective-permute-start(f32[2,128]{1,0:T(2,128)S(1)} %broadcast_in_dim.11), channel_id=1, source_target_pairs={{0,16},{8,24},{16,0},{24,8},{1,17},{9,25},{17,1},{25,9},{2,18},{10... | collective-permute-start | bytes 3080 | tf_op jit(solution)/shard_map/ppermute | solution.py:25
  143.5 4.5 %collective-permute-start.19 = (f32[2,128]{1,0:T(2,128)S(1)}, f32[2,128]{1,0:T(2,128)S(1)}, u32[]{:S(2)}, u32[]{:S(2)}) collective-permute-start(f32[2,128]{1,0:T(2,128)S(1)} %broadcast_in_dim.11), channel_id=1, source_target_pairs={{0,24},{8,16},{16,8},{24,0},{1,25},{9,17},{17,9},{25,1},{2,26},{10... | collective-permute-start | bytes 3080 | tf_op jit(solution)/shard_map/ppermute | solution.py:25
  150.0 1.2 copy-start.5
  151.4 21.0 %collective-permute-start.27 = (bf16[2,1,256,512]{3,2,1,0:T(8,128)(2,1)S(1)}, bf16[2,1,256,512]{3,2,1,0:T(8,128)(2,1)S(1)}, u32[]{:S(2)}, u32[]{:S(2)}) collective-permute-start(bf16[2,1,256,512]{3,2,1,0:T(8,128)(2,1)S(1)} %combine.7), channel_id=1, source_target_pairs={{0,8},{8,0},{16,24},{24,16},{1,9},{9,1},{17,25},{25,17},{2,10},{10... | collective-permute-start | bytes 1572872 | tf_op jit(solution)/shard_map/ppermute | solution.py:25
  152.0 1.2 copy-start.3
  153.4 19.1 %collective-permute-start.25 = (bf16[2,1,256,512]{3,2,1,0:T(8,128)(2,1)S(1)}, bf16[2,1,256,512]{3,2,1,0:T(8,128)(2,1)S(1)}, u32[]{:S(2)}, u32[]{:S(2)}) collective-permute-start(bf16[2,1,256,512]{3,2,1,0:T(8,128)(2,1)S(1)} %combine.6), channel_id=1, source_target_pairs={{0,16},{8,24},{16,0},{24,8},{1,17},{9,25},{17,1},{25,9},{2,18},{10... | collective-permute-start | bytes 1572872 | tf_op jit(solution)/shard_map/ppermute | solution.py:25
  155.0 1.2 copy-start.1
  157.3 15.1 %collective-permute-start.23 = (bf16[2,1,256,512]{3,2,1,0:T(8,128)(2,1)S(1)}, bf16[2,1,256,512]{3,2,1,0:T(8,128)(2,1)S(1)}, u32[]{:S(2)}, u32[]{:S(2)}) collective-permute-start(bf16[2,1,256,512]{3,2,1,0:T(8,128)(2,1)S(1)} %combine.5), channel_id=1, source_target_pairs={{0,8},{8,0},{16,24},{24,16},{1,9},{9,1},{17,25},{25,17},{2,10},{10... | collective-permute-start | bytes 1572872 | tf_op jit(solution)/shard_map/ppermute | solution.py:25
  160.0 14.1 %collective-permute-start.21 = (bf16[2,1,256,512]{3,2,1,0:T(8,128)(2,1)S(1)}, bf16[2,1,256,512]{3,2,1,0:T(8,128)(2,1)S(1)}, u32[]{:S(2)}, u32[]{:S(2)}) collective-permute-start(bf16[2,1,256,512]{3,2,1,0:T(8,128)(2,1)S(1)} %combine.4), channel_id=1, source_target_pairs={{0,16},{8,24},{16,0},{24,8},{1,17},{9,25},{17,1},{25,9},{2,18},{10... | collective-permute-start | bytes 1572872 | tf_op jit(solution)/shard_map/ppermute | solution.py:25
  160.6 13.6 %copy-start.2 = (bf16[2,2,256,512]{3,2,1,0:T(8,128)(2,1)S(1)}, bf16[2,2,256,512]{3,2,1,0:T(8,128)(2,1)}, u32[]{:S(2)}) copy-start(bf16[2,2,256,512]{3,2,1,0:T(8,128)(2,1)} %get-tuple-element.43.refs_0_.refs_3_) | copy-start | bytes 3145732
  160.6 13.6 %copy-start.4 = (bf16[2,2,256,512]{3,2,1,0:T(8,128)(2,1)S(1)}, bf16[2,2,256,512]{3,2,1,0:T(8,128)(2,1)}, u32[]{:S(2)}) copy-start(bf16[2,2,256,512]{3,2,1,0:T(8,128)(2,1)} %get-tuple-element.45.refs_0_.refs_6_) | copy-start | bytes 3145732
  160.6 13.6 %copy-start.6 = (bf16[2,2,256,512]{3,2,1,0:T(8,128)(2,1)S(1)}, bf16[2,2,256,512]{3,2,1,0:T(8,128)(2,1)}, u32[]{:S(2)}) copy-start(bf16[2,2,256,512]{3,2,1,0:T(8,128)(2,1)} %get-tuple-element.47.refs_0_.refs_9_) | copy-start | bytes 3145732
where the time goes:
time: 179 us; the launch traced here: 178 us
  waiting for transfers between devices  56.4 us (32%)
  Pallas kernels  52.3 us (29%)
  starting transfers between devices  32.4 us (18%)
  other arithmetic  27.6 us (15%)
  local copies, waits for them, and re-layouts  6.59 us (4%)
  between operations  3.01 us (2%)
    ppermute x28, waiting for transfers between devices, swap(): return lax.ppermute(x, axis, partners(lax.axis_size(axis), flip))  56.4 us
    ppermute x28, starting transfers between devices, swap(): return lax.ppermute(x, axis, partners(lax.axis_size(axis), flip))  32.4 us
    pallas_call x4, Pallas kernels, update_chunk(): pl.pallas_call(functools.partial(update_kernel, (send, keep)), grid=(grou...  27.2 us
    pallas_call x2, Pallas kernels, statistics(): pl.pallas_call(functools.partial(kernel, blocks), in_specs=[LEFT] * len(b...  18.1 us
    add x1, other arithmetic, program(): outer_new = outer_weight + outer_update  11.9 us
    reduce_sum x1, other arithmetic, program(): outer_weight_sq = jnp.sum(outer_weight * outer_weight)  6.14 us
    reduce_sum x1, other arithmetic, program(): col_sum = jnp.sum(outer_sq + 1e-30, axis=0)  4.17 us
    pallas_call x1, Pallas kernels, finish(): pl.pallas_call(functools.partial(final_kernel, [len(chunk) for chunk in c...  4.13 us
  transfers between devices with their start and end apart: 28, of which 10 were waited for; matrix products, arithmetic and copies ran while one was open for 17% of the time, Pallas kernels for 17%

commit v1 on v0

--- a/solution.py
+++ b/solution.py
@@ -86,7 +86,7 @@
     return copies, height
 
 
-def col_kernel(blocks, grad_ref, sum_ref, held, sems):
+def col_kernel(floor, blocks, grad_ref, sum_ref, held, sems):
     groups, depth, columns = held.shape
     copies, height = fetch(grad_ref, held, sems, blocks)
     for group in range(groups):
@@ -99,7 +99,7 @@
                 return sums + value * value
 
             sums = lax.fori_loop(0, height // 8, add, sums, unroll=4)
-        sum_ref[group : group + 1, :] = jnp.sum(sums, axis=0, keepdims=True) + depth * 1e-30
+        sum_ref[group : group + 1, :] = jnp.sum(sums, axis=0, keepdims=True) + depth * floor
 
 
 def row_kernel(blocks, grad_ref, weight_ref, inverse_ref, packed_ref, held, weights, plain_ref, over_ref, sems, more):
@@ -137,6 +137,35 @@
         packed_ref[group : group + 1, :depth] = across(plain_ref[...])[:1] + columns * 1e-30
         packed_ref[group : group + 1, depth : 2 * depth] = across(over_ref[...])[:1]
         packed_ref[group : group + 1, 2 * depth :] = jnp.full((1, 128), jnp.sum(sums), jnp.float32)
+
+
+def outer_kernel(blocks, grad_ref, weight_ref, row_ref, packed_ref, held, weights, spread, sems, more):
+    _, depth, columns = held.shape
+    copies, height = fetch(grad_ref, held, sems, blocks, False)
+    weight_copies, _ = fetch(weight_ref, weights, more, blocks, False)
+    for pair in zip(copies, weight_copies):
+        for copy in pair:
+            copy.start()
+    for start in range(0, depth, 128):
+        factor = 1.0 / row_ref[:, start : start + 128]
+        spread[start : start + 128, :] = jnp.broadcast_to(factor, (128, 128)).T
+    sums = (jnp.zeros((8, columns), jnp.float32),) * 3
+    for block in range(blocks):
+        copies[block].wait()
+        weight_copies[block].wait()
+
+        def add(i, sums):
+            at = pl.ds(pl.multiple_of(block * height + i * 8, 8), 8)
+            square = held[0, at, :] * held[0, at, :]
+            weight = weights[0, at, :]
+            over = square * jnp.concatenate([spread[at, :]] * (columns // 128), axis=1)
+            return sums[0] + square, sums[1] + over, sums[2] + weight * weight
+
+        sums = lax.fori_loop(0, height // 8, add, sums, unroll=4)
+    packed_ref[:, :columns] = jnp.sum(sums[0], axis=0, keepdims=True) + depth * 1e-30
+    packed_ref[:, columns : 2 * columns] = jnp.sum(sums[1], axis=0, keepdims=True)
+    packed_ref[:, 2 * columns : 2 * columns + 128] = jnp.full((1, 128), jnp.sum(sums[2]), jnp.float32)
+    packed_ref[:, 2 * columns + 128 :] = jnp.full((1, 128), jnp.sum(row_ref[...]), jnp.float32)
 
 
 def statistics(kernel, bigs, small, out, more):
@@ -181,31 +210,29 @@
     groups, depth, _ = grad.shape
     count = len(send) + len(keep)
     rows = tokens[0].shape[0]
-    step = min(512, width)
-    first = start // step
-    cols = lambda g, j: (g, 0, first + j)
-    whole = pl.BlockSpec((1, depth, step), cols)
-    part = lambda count: pl.BlockSpec((1, count, rows, step), lambda g, j: (g, 0, 0, j))
+    cols = lambda g: (g, 0, start)
+    whole = pl.BlockSpec((pl.Element(1), pl.Element(depth), pl.Element(width)), cols)
+    part = lambda count: pl.BlockSpec((1, count, rows, width), lambda g: (g, 0, 0, 0))
     out = lambda count: pltpu.HBM((groups, count, rows, width), jnp.bfloat16)
     big = jax.ShapeDtypeStruct(grad.shape, jnp.float32)
     extra = [] if held is None else list(held)
     return pl.pallas_call(
         functools.partial(update_kernel, (send, keep)),
-        grid=(groups, width // step),
+        grid=(groups,),
         in_specs=[
             pl.BlockSpec(memory_space=pltpu.SMEM),
-            pl.BlockSpec((1, depth, 128), lambda g, j: (g, 0, 0)),
-            pl.BlockSpec((1, 1, step), cols),
+            pl.BlockSpec((1, depth, 128), lambda g: (g, 0, 0)),
+            pl.BlockSpec((pl.Element(1), pl.Element(1), pl.Element(width)), cols),
             whole,
             whole,
-            *[pl.BlockSpec(piece.shape, lambda g, j: (0, 0)) for piece in tokens],
+            *[pl.BlockSpec(piece.shape, lambda g: (0, 0)) for piece in tokens],
             *[LEFT for _ in extra],
         ],
         out_specs=[whole, whole, part(len(send)), part(len(keep))],
         out_shape=[big, big, out(len(send)), out(len(keep))],
-        scratch_shapes=[pltpu.VMEM((depth, step), jnp.bfloat16)],
+        scratch_shapes=[pltpu.VMEM((depth, width), jnp.bfloat16)],
         input_output_aliases={5 + count: 0, 6 + count: 1} if extra else {},
-        compiler_params=pltpu.CompilerParams(vmem_limit_bytes=LIMIT),
+        compiler_params=pltpu.CompilerParams(vmem_limit_bytes=max(LIMIT, (LIMIT >> 9) * width)),
         cost_estimate=pl.CostEstimate(
             flops=2 * count * rows * depth * width * groups,
             bytes_accessed=groups * width * (16 * depth + 2 * count * rows),
@@ -272,33 +299,39 @@
         place, start = place + count, start + width
 
 
-def finish(chunks):
-    rows = chunks[0][0][0].shape[2]
+def finish(chunks, hidden, start, shape):
+    rows = shape[0]
     columns = sum(terms[0][0].shape[3] for terms in chunks)
-    height = rows // 4
+    height = rows // 2
     terms = [term for chunk in chunks for term in chunk]
     spec = lambda value, place: pl.BlockSpec((2, 1, height, value.shape[3]), lambda i: (0, place, i, 0))
+    extra = [] if hidden is None else [hidden]
     return pl.pallas_call(
         functools.partial(final_kernel, [len(chunk) for chunk in chunks]),
         grid=(rows // height,),
-        in_specs=[spec(value, place) for value, place in terms],
-        out_specs=pl.BlockSpec((height, columns), lambda i: (i, 0)),
-        out_shape=jax.ShapeDtypeStruct((rows, columns), jnp.bfloat16),
+        in_specs=[spec(value, place) for value, place in terms] + [LEFT for _ in extra],
+        out_specs=pl.BlockSpec((pl.Element(height), pl.Element(columns)), lambda i: (i * height, start)),
+        out_shape=jax.ShapeDtypeStruct(shape, jnp.bfloat16),
+        input_output_aliases={len(terms): 0} if extra else {},
         compiler_params=pltpu.CompilerParams(vmem_limit_bytes=LIMIT),
-        cost_estimate=pl.CostEstimate(
-            flops=0, bytes_accessed=20 * rows * columns, transcendentals=rows * columns
-        ),
+        cost_estimate=pl.CostEstimate(flops=0, bytes_accessed=20 * rows * columns, transcendentals=rows * columns),
         name="finish",
-    )(*[value for value, _ in terms])
+    )(*[value for value, _ in terms], *extra)
 
 
 def plan(columns, count):
     bits = bits_of(count)
-    pieces = min(4, columns // 128)
-    width = columns // pieces
-    return [
-        (i * width, width, bits[i % len(bits) :] + bits[: i % len(bits)]) for i in range(pieces)
-    ]
+    units = columns // 128
+    widths = [units // 4, units * 3 // 16, units - 2 * (units // 4) - units * 3 // 16, units // 4]
+    if units % 16 or len(bits) < 2:
+        widths = [units - units // 2, units // 2]
+    chunks, start = [], 0
+    for i, width in enumerate(widths):
+        turn = i % max(1, len(bits))
+        if width:
+            chunks.append((start * 128, width * 128, bits[turn:] + bits[:turn]))
+        start += width
+    return chunks
 
 
 def split(blocks, bit):
@@ -311,26 +344,27 @@
     data_count = lax.axis_size("dp")
     data_index = lax.axis_index("dp")
     groups, depth, columns = inner_grad.shape
+    rows = tokens.shape[0]
     sum_data = lambda v: total(v, "dp", rounds("dp", (4,)))
     sum_model = lambda v: total(v, "mp", rounds("mp", (2,)))
 
-    col_part = statistics(col_kernel, (inner_grad,), (), (groups, columns), ())
+    col_part = statistics(functools.partial(col_kernel, 1e-30), (inner_grad,), (), (groups, columns), ())
     col_sum = sum_data(col_part)
     inner_col_new = FORGET * inner_col + FRESH * (col_sum / D)
     inverse_col = 1.0 / inner_col_new
     tokens_late = tie(tokens, col_part)
     share = []
     for flip in range(data_count):
-        piece = lax.dynamic_slice_in_dim(tokens_late, (data_index ^ flip) * depth, depth, 1)
-        share.append(piece if flip == 0 else swap(piece, "dp", flip))
+        if flip:
+            piece = lax.dynamic_slice_in_dim(tokens_late, (data_index ^ flip) * depth, depth, 1)
+            share.append(swap(piece, "dp", flip))
 
     columned = [pltpu.VMEM((depth, 128), jnp.float32)] * 2
     packed = statistics(row_kernel, (inner_grad, inner_weight), (inverse_col,), (groups, 2 * depth + 128), columned)
+    share = [lax.dynamic_slice_in_dim(tie(tokens, packed), data_index * depth, depth, 1), *share]
     outer_grad = tie(outer_grad, packed)
     outer_sq = outer_grad * outer_grad
     outer_part = jnp.sum(outer_sq + 1e-30, axis=1)
-    outer_weight = tie(outer_weight, packed)
-    outer_weight_sq = jnp.sum(outer_weight * outer_weight)
     packed = sum_model(packed)
     row_sum, weighted, weight_sq = packed[:, :depth], packed[:, depth : 2 * depth], packed[:, 2 * depth]
     inner_row_new = FORGET * inner_row + FRESH * (row_sum / FF)
@@ -364,16 +398,19 @@
             came = swap(sent, "dp", order[level])
             later.append((start, width, order, keep, [*terms, (came, keep)]))
         chunks = later
-    hidden = finish([[(value, names.index(0)) for value, names in terms] for *_, terms in chunks])
+    hidden, half = None, len(chunks) // 2
+    for group in (chunks[:half], chunks[half:]):
+        if group:
+            terms = [[(value, names.index(0)) for value, names in terms] for *_, terms in group]
+            hidden = finish(terms, hidden, group[0][0], (rows, columns))
 
     outer_row_new = FORGET * outer_row + FRESH * (outer_row_sum / D)
-    outer_grad = tie(outer_grad, outer_row_new)
-    outer_sq = outer_grad * outer_grad
-    col_sum = jnp.sum(outer_sq + 1e-30, axis=0)
-    weighted = jnp.sum(outer_sq * (1.0 / outer_row_new)[:, None], axis=0)
-    spare = jnp.broadcast_to(jnp.stack([outer_weight_sq, jnp.sum(outer_row_new)])[:, None], (2, 128)).reshape(-1)
-    packed = jnp.concatenate([col_sum, weighted, spare])
-    packed = sum_model(packed)
+    outer_grad, outer_weight = tie(outer_grad, outer_row_new), tie(outer_weight, outer_row_new)
+    depth, columns = outer_grad.shape
+    spread = (pltpu.VMEM((depth, 128), jnp.float32),)
+    bigs = (outer_grad[None], outer_weight[None])
+    packed = statistics(outer_kernel, bigs, (outer_row_new[None],), (1, 2 * columns + 256), spread)
+    packed = sum_model(packed)[0]
     width = outer_col.shape[0]
     outer_col_new = FORGET * outer_col + FRESH * (packed[:width] / FF)
     scalars = jnp.stack([jnp.sum(packed[width : 2 * width] / outer_col_new), packed[2 * width]])

time: 179 us -> 178 us (level)
  waiting for transfers between devices: 56.4 us -> 65.5 us
  other arithmetic: 27.6 us -> 18.7 us
  Pallas kernels: 52.3 us -> 57.1 us
  starting transfers between devices: 32.4 us -> 28.4 us
    reduce_sum x2 -> x0, other arithmetic: 10.3 us -> none  [the longest x1 6.14 us: program(): outer_weight_sq = jnp.sum(outer_weight * outer_weight)]
    ppermute x28, waiting for transfers between devices: 56.4 us -> 65.5 us  [swap(): return lax.ppermute(x, axis, partners(lax.axis_size(axis), flip))]
    pallas_call x2 -> x3, Pallas kernels: 18.1 us -> 24.4 us  [statistics(): pl.pallas_call(functools.partial(kernel, blocks), in_specs=[LEFT] * len(b...]
    ppermute x28, starting transfers between devices: 32.4 us -> 28.4 us  [swap(): return lax.ppermute(x, axis, partners(lax.axis_size(axis), flip))]
    reduce_sum x1, other arithmetic: 0.89 us -> 4.27 us  [program(): outer_part = jnp.sum(outer_sq + 1e-30, axis=1)]
    unnamed x34 -> x30, local copies, waits for them, and re-layouts: 3.74 us -> 1.3 us
    pallas_call x4, Pallas kernels: 2.52 us -> 0.63 us  [combine(): pl.pallas_call(functools.partial(combine_kernel, len(terms)), grid=(group...]
    pallas_call x1 -> x2, Pallas kernels: 4.13 us -> 3.48 us  [finish(): pl.pallas_call(functools.partial(final_kernel, [len(chunk) for chunk in c...]
  transfers between devices with their start and end apart: 28 -> 28, of which waited for: 10 -> 13; matrix products, arithmetic and copies ran while one was open for 17% -> 13% of each run, Pallas kernels for 17% -> 17%
where the time goes in v1:
time: 178 us
  waiting for transfers between devices  65.5 us (37%)
  Pallas kernels  57.1 us (32%)
  starting transfers between devices  28.4 us (16%)
  other arithmetic  18.7 us (11%)
  local copies, waits for them, and re-layouts  5.13 us (3%)
  between operations  3.15 us (2%)
    ppermute x28, waiting for transfers between devices, swap(): return lax.ppermute(x, axis, partners(lax.axis_size(axis), flip))  65.5 us
    ppermute x28, starting transfers between devices, swap(): return lax.ppermute(x, axis, partners(lax.axis_size(axis), flip))  28.4 us
    pallas_call x4, Pallas kernels, update_chunk(): pl.pallas_call(functools.partial(update_kernel, (send, keep)), grid=(grou...  28.2 us
    pallas_call x3, Pallas kernels, statistics(): pl.pallas_call(functools.partial(kernel, blocks), in_specs=[LEFT] * len(b...  24.4 us
    add x1, other arithmetic, program(): outer_new = outer_weight + outer_update  11.8 us
    reduce_sum x1, other arithmetic, program(): outer_part = jnp.sum(outer_sq + 1e-30, axis=1)  4.27 us
  transfers between devices with their start and end apart: 28, of which 13 were waited for; matrix products, arithmetic and copies ran while one was open for 13% of the time, Pallas kernels for 17%

profile of v1, /device:TPU:0, one launch (start us, length us, event | category | flops | bytes accessed | tf_op | source)
XLA Modules:
  0.0 178.0 jit_solution(11299938694650924635)
XLA Ops:
  0.7 6.1 %shard_map.160 = f32[2,2048]{1,0:T(2,128)S(1)} custom-call(f32[2,1024,2048]{2,1,0:T(8,128)} %grad_ref.11), custom_call_target="tpu_custom_call" | custom-call | flops 16777216 | bytes 16777216 | tf_op jit(solution)/shard_map/pallas_call | solution.py:176
  6.7 3.0 %collective-permute-start = (f32[2,2048]{1,0:T(2,128)S(1)}, f32[2,2048]{1,0:T(2,128)S(1)}, u32[]{:S(2)}, u32[]{:S(2)}) collective-permute-start(f32[2,2048]{1,0:T(2,128)S(1)} %shard_map.160), channel_id=1, source_target_pairs={{0,8},{8,0},{16,24},{24,16},{1,9},{9,1},{17,25},{25,17},{2,10},{10... | collective-permute-start | bytes 49160 | tf_op jit(solution)/shard_map/ppermute | solution.py:25
  9.7 1.5 collective-permute-start.1
  11.3 0.2 collective-permute-done
  11.5 2.0 %collective-permute-done.1 = f32[2,2048]{1,0:T(2,128)S(1)} collective-permute-done((f32[2,2048]{1,0:T(2,128)S(1)}, f32[2,2048]{1,0:T(2,128)S(1)}, u32[]{:S(2)}, u32[]{:S(2)}) %collective-permute-start.1) | collective-permute-done | bytes 16416 | tf_op jit(solution)/shard_map/ppermute | solution.py:25
  13.5 2.4 %collective-permute-done.2 = f32[2,2048]{1,0:T(2,128)S(1)} collective-permute-done((f32[2,2048]{1,0:T(2,128)S(1)}, f32[2,2048]{1,0:T(2,128)S(1)}, u32[]{:S(2)}, u32[]{:S(2)}) %collective-permute-start.2) | collective-permute-done | bytes 16416 | tf_op jit(solution)/shard_map/ppermute | solution.py:25
  16.0 12.0 %shard_map.161 = f32[2,2176]{1,0:T(2,128)S(1)} custom-call(f32[2,1024,2048]{2,1,0:T(8,128)} %grad_ref.11, f32[2,1024,2048]{2,1,0:T(8,128)} %weight_ref.9, f32[2,2048]{1,0:T(2,128)S(1)} %broadcast_divide_fusion.inverse_ref), custom_call_target="tpu_custom_call" | custom-call | flops 33554432 | bytes 33554432 | tf_op jit(solution)/shard_map/pallas_call | solution.py:176
  28.1 1.1 constant_dynamic-slice_fusion
  29.2 0.5 collective-permute-start.10
  29.8 2.1 %collective-permute-start.4 = (f32[2,2176]{1,0:T(2,128)S(1)}, f32[2,2176]{1,0:T(2,128)S(1)}, u32[]{:S(2)}, u32[]{:S(2)}) collective-permute-start(f32[2,2176]{1,0:T(2,128)S(1)} %add.90), channel_id=1, source_target_pairs={{0,2},{1,3},{2,0},{3,1},{4,6},{5,7},{6,4},{7,5},{8,10},{9,11},{10,... | collective-permute-start | bytes 52232 | tf_op jit(solution)/shard_map/ppermute | solution.py:25
  31.9 2.6 %collective-permute-start.5 = (f32[2,2176]{1,0:T(2,128)S(1)}, f32[2,2176]{1,0:T(2,128)S(1)}, u32[]{:S(2)}, u32[]{:S(2)}) collective-permute-start(f32[2,2176]{1,0:T(2,128)S(1)} %add.90), channel_id=1, source_target_pairs={{0,4},{1,5},{2,6},{3,7},{4,0},{5,1},{6,2},{7,3},{8,12},{9,13},{10,... | collective-permute-start | bytes 52232 | tf_op jit(solution)/shard_map/ppermute | solution.py:25
  34.5 4.3 %add_reduce_fusion = f32[2048]{0:T(1024)S(1)} fusion(f32[2048,1024]{1,0:T(8,128)} %param.15), kind=kLoop, calls=%fused_computation.1 | loop fusion | flops 6289408 | bytes 8396800 | tf_op jit(solution)/shard_map/reduce_sum | solution.py:367
  38.8 1.3 collective-permute-done.6
  40.1 0.2 fusion.3
  40.3 0.1 copy.29
  40.4 0.1 copy.30
  40.5 0.1 pad_maximum_fusion.1
  40.6 1.5 collective-permute-start.7
  42.2 1.5 collective-permute-start.8
  43.7 0.5 collective-permute-start.9
  44.2 1.1 constant_dynamic-slice_fusion.3.refs_0_
  45.3 0.3 spread_rows.1.row_ref
  45.6 0.2 collective-permute-done.8
  45.9 2.4 %collective-permute-done.9 = f32[2816]{0:T(1024)S(1)} collective-permute-done((f32[2816]{0:T(1024)S(1)}, f32[2816]{0:T(1024)S(1)}, u32[]{:S(2)}, u32[]{:S(2)}) %collective-permute-start.9) | collective-permute-done | bytes 11296 | tf_op jit(solution)/shard_map/ppermute | solution.py:25
  48.4 6.3 %shard_map.162 = f32[1,2304]{1,0:T(1,128)S(1)} custom-call(f32[1,2048,1024]{2,1,0:T(8,128)} %bitcast.11, f32[1,2048,1024]{2,1,0:T(8,128)} %bitcast.12, f32[1,2048]{1,0:T(1,128)S(1)} %bitcast.10), custom_call_target="tpu_custom_call" | custom-call | flops 16777216 | bytes 16777216 | tf_op jit(solution)/shard_map/pallas_call | solution.py:176
  54.8 0.1 slice_reduce_fusion
  54.9 1.1 collective-permute-done.13
  56.0 3.1 %collective-permute-start.15 = (f32[1,2304]{1,0:T(1,128)S(1)}, f32[1,2304]{1,0:T(1,128)S(1)}, u32[]{:S(2)}, u32[]{:S(2)}) collective-permute-start(f32[1,2304]{1,0:T(1,128)S(1)} %add.103), channel_id=1, source_target_pairs={{0,4},{1,5},{2,6},{3,7},{4,0},{5,1},{6,2},{7,3},{8,12},{9,13},{10,... | collective-permute-start | bytes 27656 | tf_op jit(solution)/shard_map/ppermute | solution.py:25
  59.2 1.2 collective-permute-start.16
  60.4 0.2 multiply_reduce_fusion.coef
  60.6 0.5 collective-permute-start.12
  61.2 3.5 %collective-permute-done.16 = f32[1,2304]{1,0:T(1,128)S(1)} collective-permute-done((f32[1,2304]{1,0:T(1,128)S(1)}, f32[1,2304]{1,0:T(1,128)S(1)}, u32[]{:S(2)}, u32[]{:S(2)}) %collective-permute-start.16) | collective-permute-done | bytes 9248 | tf_op jit(solution)/shard_map/ppermute | solution.py:25
  64.7 10.1 %collective-permute-done.12.refs_3_ = bf16[256,1024]{1,0:T(8,128)(2,1)S(1)} collective-permute-done((bf16[256,1024]{1,0:T(8,128)(2,1)S(1)}, bf16[256,1024]{1,0:T(8,128)(2,1)S(1)}, u32[]{:S(2)}, u32[]{:S(2)}) %collective-permute-start.12) | collective-permute-done | bytes 524320 | tf_op jit(solution)/shard_map/ppermute | solution.py:25
  74.7 6.8 %update_chunk.4 = (f32[2,1024,2048]{2,1,0:T(8,128)}, f32[2,1024,2048]{2,1,0:T(8,128)}, bf16[2,2,256,512]{3,2,1,0:T(8,128)(2,1)}, bf16[2,2,256,512]{3,2,1,0:T(8,128)(2,1)}) custom-call(f32[2]{0:T(128)S(1)} %multiply_reduce_fusion.coef, f32[2,1024,128]{2,1,0:T(8,128)S(1)} %spread_rows.1.row_ref, f32[2,1,2048]{2,1,0:T(1,128)S(1)} %broadcast_in_dim.13.col_ref, ...), custom_call_target="tpu_custom_call" | custom-call | flops 2147483648 | bytes 18874368 | tf_op jit(solution)/shard_map/update_chunk/pallas_call | solution.py:219
  81.5 0.5 collective-permute-start.24
  82.0 6.3 %update_chunk.5 = (f32[2,1024,2048]{2,1,0:T(8,128)}, f32[2,1024,2048]{2,1,0:T(8,128)}, bf16[2,2,256,384]{3,2,1,0:T(8,128)(2,1)}, bf16[2,2,256,384]{3,2,1,0:T(8,128)(2,1)}) custom-call(f32[2]{0:T(128)S(1)} %multiply_reduce_fusion.coef, f32[2,1024,128]{2,1,0:T(8,128)S(1)} %spread_rows.1.row_ref, ...), custom_call_target="tpu_custom_call", output_to_operand_aliasing={{0}: (9, {}), {1}: (10, {})} | custom-call | flops 1610612736 | bytes 14155776 | tf_op jit(solution)/shard_map/update_chunk/pallas_call | solution.py:219
  88.3 8.1 %update_chunk.6 = (f32[2,1024,2048]{2,1,0:T(8,128)}, f32[2,1024,2048]{2,1,0:T(8,128)}, bf16[2,2,256,640]{3,2,1,0:T(8,128)(2,1)}, bf16[2,2,256,640]{3,2,1,0:T(8,128)(2,1)}) custom-call(f32[2]{0:T(128)S(1)} %multiply_reduce_fusion.coef, f32[2,1024,128]{2,1,0:T(8,128)S(1)} %spread_rows.1.row_ref, ...), custom_call_target="tpu_custom_call", output_to_operand_aliasing={{0}: (9, {}), {1}: (10, {})} | custom-call | flops 2684354560 | bytes 23592960 | tf_op jit(solution)/shard_map/update_chunk/pallas_call | solution.py:219
  96.4 1.5 collective-permute-start.20
  97.9 7.1 %update_chunk.7 = (f32[2,1024,2048]{2,1,0:T(8,128)}, f32[2,1024,2048]{2,1,0:T(8,128)}, bf16[2,2,256,512]{3,2,1,0:T(8,128)(2,1)}, bf16[2,2,256,512]{3,2,1,0:T(8,128)(2,1)}) custom-call(f32[2]{0:T(128)S(1)} %multiply_reduce_fusion.coef, f32[2,1024,128]{2,1,0:T(8,128)S(1)} %spread_rows.1.row_ref, ...), custom_call_target="tpu_custom_call", output_to_operand_aliasing={{0}: (9, {}), {1}: (10, {})} | custom-call | flops 2147483648 | bytes 18874368 | tf_op jit(solution)/shard_map/update_chunk/pallas_call | solution.py:219
  105.0 0.5 collective-permute-start.22
  105.5 0.7 divide_reduce_fusion
  106.2 1.5 collective-permute-start.26
  107.8 0.6 fusion.9
  108.4 1.3 pad_maximum_fusion.2
  109.7 0.5 collective-permute-start.17
  110.3 23.1 %collective-permute-done.17 = f32[2,128]{1,0:T(2,128)S(1)} collective-permute-done((f32[2,128]{1,0:T(2,128)S(1)}, f32[2,128]{1,0:T(2,128)S(1)}, u32[]{:S(2)}, u32[]{:S(2)}) %collective-permute-start.17) | collective-permute-done | bytes 1056 | tf_op jit(solution)/shard_map/ppermute | solution.py:25
  133.4 0.5 collective-permute-start.18
  133.9 11.2 %collective-permute-done.18 = f32[2,128]{1,0:T(2,128)S(1)} collective-permute-done((f32[2,128]{1,0:T(2,128)S(1)}, f32[2,128]{1,0:T(2,128)S(1)}, u32[]{:S(2)}, u32[]{:S(2)}) %collective-permute-start.18) | collective-permute-done | bytes 1056 | tf_op jit(solution)/shard_map/ppermute | solution.py:25
  145.1 0.5 collective-permute-start.19
  146.3 3.3 %collective-permute-done.19 = f32[2,128]{1,0:T(2,128)S(1)} collective-permute-done((f32[2,128]{1,0:T(2,128)S(1)}, f32[2,128]{1,0:T(2,128)S(1)}, u32[]{:S(2)}, u32[]{:S(2)}) %collective-permute-start.19) | collective-permute-done | bytes 1056 | tf_op jit(solution)/shard_map/ppermute | solution.py:25
  149.7 0.6 fusion.10
  151.7 0.1 combine.7
  151.8 0.6 collective-permute-start.27
  152.5 0.1 combine.6
  152.6 0.6 collective-permute-start.25
  153.2 1.2 copy-done.1
  154.4 0.1 combine.5
  154.6 1.6 collective-permute-start.23
  156.1 0.2 combine.4
  156.3 1.6 collective-permute-start.21
  157.9 11.8 %fusion.4 = (f32[2048,1024]{1,0:T(8,128)}, f32[2048,1024]{1,0:T(8,128)}) fusion(f32[2048,1024]{1,0:T(8,128)} %param.14, f32[2048,1024]{1,0:T(8,128)} %param.15, f32[1024]{0:T(1024)S(1)} %rsqrt_multiply_fusion, f32[2048]{0:T(1024)S(1)} %get-tuple-element.55), kind=kLoop, calls=%fused_computation.29 | loop fusion | flops 6291456 | bytes 33566720 | tf_op jit(solution)/shard_map/add | solution.py:423
  169.7 1.6 finish.2.refs_6_
  171.4 4.8 %collective-permute-done.21.refs_2_ = bf16[2,1,256,640]{3,2,1,0:T(8,128)(2,1)S(1)} collective-permute-done((bf16[2,1,256,640]{3,2,1,0:T(8,128)(2,1)S(1)}, bf16[2,1,256,640]{3,2,1,0:T(8,128)(2,1)S(1)}, u32[]{:S(2)}, u32[]{:S(2)}) %collective-permute-start.21) | collective-permute-done | bytes 655392 | tf_op jit(solution)/shard_map/ppermute | solution.py:25
  176.1 1.9 %finish.3 = bf16[256,2048]{1,0:T(8,128)(2,1)} custom-call(bf16[2,2,256,640]{3,2,1,0:T(8,128)(2,1)S(1)} %copy-done, bf16[2,2,256,640]{3,2,1,0:T(8,128)(2,1)S(1)} %collective-permute-done.20.refs_1_, bf16[2,1,256,640]{3,2,1,0:T(8,128)(2,1)S(1)} %collective-permute-done.21.refs_2_, ...), custom_call_target="tpu_custom_call", output_to_operand_aliasing={{}: (6, {})} | custom-call | bytes 5898240 | tf_op jit(solution)/shard_map/finish/pallas_call | solution.py:309
  (69 shorter events, 0.8 us)
Async XLA Ops:
  0.6 15.3 %copy-start.9 = (f32[2,2048]{1,0:T(2,128)S(1)}, f32[2,2048]{1,0:T(2,128)}, u32[]{:S(2)}) copy-start(f32[2,2048]{1,0:T(2,128)} %param.13) | copy-start | bytes 49156
  6.7 4.8 %collective-permute-start = (f32[2,2048]{1,0:T(2,128)S(1)}, f32[2,2048]{1,0:T(2,128)S(1)}, u32[]{:S(2)}, u32[]{:S(2)}) collective-permute-start(f32[2,2048]{1,0:T(2,128)S(1)} %shard_map.160), channel_id=1, source_target_pairs={{0,8},{8,0},{16,24},{24,16},{1,9},{9,1},{17,25},{25,17},{2,10},{10... | collective-permute-start | bytes 49160 | tf_op jit(solution)/shard_map/ppermute | solution.py:25
  9.7 3.7 %collective-permute-start.1 = (f32[2,2048]{1,0:T(2,128)S(1)}, f32[2,2048]{1,0:T(2,128)S(1)}, u32[]{:S(2)}, u32[]{:S(2)}) collective-permute-start(f32[2,2048]{1,0:T(2,128)S(1)} %shard_map.160), channel_id=1, source_target_pairs={{0,16},{8,24},{16,0},{24,8},{1,17},{9,25},{17,1},{25,9},{2,18},{10... | collective-permute-start | bytes 49160 | tf_op jit(solution)/shard_map/ppermute | solution.py:25
  11.3 4.6 %collective-permute-start.2 = (f32[2,2048]{1,0:T(2,128)S(1)}, f32[2,2048]{1,0:T(2,128)S(1)}, u32[]{:S(2)}, u32[]{:S(2)}) collective-permute-start(f32[2,2048]{1,0:T(2,128)S(1)} %shard_map.160), channel_id=1, source_target_pairs={{0,24},{8,16},{16,8},{24,0},{1,25},{9,17},{17,9},{25,1},{2,26},{10... | collective-permute-start | bytes 49160 | tf_op jit(solution)/shard_map/ppermute | solution.py:25
  15.9 12.1 %copy-start.8 = (f32[2,2048]{1,0:T(2,128)}, f32[2,2048]{1,0:T(2,128)S(1)}, u32[]{:S(2)}) copy-start(f32[2,2048]{1,0:T(2,128)S(1)} %get-tuple-element.60) | copy-start | bytes 49156
  16.0 12.1 %copy-start.7 = (bf16[256,4096]{1,0:T(8,128)(2,1)S(1)}, bf16[256,4096]{1,0:T(8,128)(2,1)}, u32[]{:S(2)}) copy-start(bf16[256,4096]{1,0:T(8,128)(2,1)} %param.9) | copy-start | bytes 6291460
  28.0 12.1 %copy-start.11 = (f32[2,1024]{1,0:T(2,128)S(1)}, f32[2,1024]{1,0:T(2,128)}, u32[]{:S(2)}) copy-start(f32[2,1024]{1,0:T(2,128)} %param.12) | copy-start | bytes 24580
  28.0 20.3 %copy-start.12 = (f32[2048]{0:T(1024)S(1)}, f32[2048]{0:T(1024)}, u32[]{:S(2)}) copy-start(f32[2048]{0:T(1024)} %param.16) | copy-start | bytes 24580
  28.0 1.8 collective-permute-start.3
  29.2 35.4 %collective-permute-start.10 = (bf16[256,1024]{1,0:T(8,128)(2,1)}, bf16[256,1024]{1,0:T(8,128)(2,1)S(1)}, u32[]{:S(2)}, u32[]{:S(2)}) collective-permute-start(bf16[256,1024]{1,0:T(8,128)(2,1)} %get-tuple-element.64), channel_id=1, source_target_pairs={{0,8},{8,0},{16,24},{24,16},{1,9},{9,1},{17,25},{25,17},{2,10},{10... | collective-permute-start | bytes 1572872 | tf_op jit(solution)/shard_map/ppermute | solution.py:25
  29.8 34.9 %collective-permute-start.11 = (bf16[256,1024]{1,0:T(8,128)(2,1)}, bf16[256,1024]{1,0:T(8,128)(2,1)S(1)}, u32[]{:S(2)}, u32[]{:S(2)}) collective-permute-start(bf16[256,1024]{1,0:T(8,128)(2,1)} %get-tuple-element.63), channel_id=1, source_target_pairs={{0,16},{8,24},{16,0},{24,8},{1,17},{9,25},{17,1},{25,9},{2,18},{10... | collective-permute-start | bytes 1572872 | tf_op jit(solution)/shard_map/ppermute | solution.py:25
  29.8 9.0 %collective-permute-start.4 = (f32[2,2176]{1,0:T(2,128)S(1)}, f32[2,2176]{1,0:T(2,128)S(1)}, u32[]{:S(2)}, u32[]{:S(2)}) collective-permute-start(f32[2,2176]{1,0:T(2,128)S(1)} %add.90), channel_id=1, source_target_pairs={{0,2},{1,3},{2,0},{3,1},{4,6},{5,7},{6,4},{7,5},{8,10},{9,11},{10,... | collective-permute-start | bytes 52232 | tf_op jit(solution)/shard_map/ppermute | solution.py:25
  31.9 6.9 %collective-permute-start.5 = (f32[2,2176]{1,0:T(2,128)S(1)}, f32[2,2176]{1,0:T(2,128)S(1)}, u32[]{:S(2)}, u32[]{:S(2)}) collective-permute-start(f32[2,2176]{1,0:T(2,128)S(1)} %add.90), channel_id=1, source_target_pairs={{0,4},{1,5},{2,6},{3,7},{4,0},{5,1},{6,2},{7,3},{8,12},{9,13},{10,... | collective-permute-start | bytes 52232 | tf_op jit(solution)/shard_map/ppermute | solution.py:25
  34.5 5.5 %collective-permute-start.6 = (f32[2,2176]{1,0:T(2,128)S(1)}, f32[2,2176]{1,0:T(2,128)S(1)}, u32[]{:S(2)}, u32[]{:S(2)}) collective-permute-start(f32[2,2176]{1,0:T(2,128)S(1)} %add.90), channel_id=1, source_target_pairs={{0,6},{1,7},{2,4},{3,5},{4,2},{5,3},{6,0},{7,1},{8,14},{9,15},{10,... | collective-permute-start | bytes 52232 | tf_op jit(solution)/shard_map/ppermute | solution.py:25
  40.3 14.4 %copy-start.6 = (f32[2,1024]{1,0:T(2,128)}, f32[2,1024]{1,0:T(2,128)S(1)}, u32[]{:S(2)}) copy-start(f32[2,1024]{1,0:T(2,128)S(1)} %get-tuple-element.61.factor_ref) | copy-start | bytes 24580
  40.6 5.0 %collective-permute-start.7 = (f32[2816]{0:T(1024)S(1)}, f32[2816]{0:T(1024)S(1)}, u32[]{:S(2)}, u32[]{:S(2)}) collective-permute-start(f32[2816]{0:T(1024)S(1)} %pad_maximum_fusion), channel_id=1, source_target_pairs={{0,8},{8,0},{16,24},{24,16},{1,9},{9,1},{17,25},{25,17},{2,10},{10... | collective-permute-start | bytes 33800 | tf_op jit(solution)/shard_map/ppermute | solution.py:25
  42.2 3.7 %collective-permute-start.8 = (f32[2816]{0:T(1024)S(1)}, f32[2816]{0:T(1024)S(1)}, u32[]{:S(2)}, u32[]{:S(2)}) collective-permute-start(f32[2816]{0:T(1024)S(1)} %pad_maximum_fusion), channel_id=1, source_target_pairs={{0,16},{8,24},{16,0},{24,8},{1,17},{9,25},{17,1},{25,9},{2,18},{10... | collective-permute-start | bytes 33800 | tf_op jit(solution)/shard_map/ppermute | solution.py:25
  43.7 4.6 %collective-permute-start.9 = (f32[2816]{0:T(1024)S(1)}, f32[2816]{0:T(1024)S(1)}, u32[]{:S(2)}, u32[]{:S(2)}) collective-permute-start(f32[2816]{0:T(1024)S(1)} %pad_maximum_fusion), channel_id=1, source_target_pairs={{0,24},{8,16},{16,8},{24,0},{1,25},{9,17},{17,9},{25,1},{2,26},{10... | collective-permute-start | bytes 33800 | tf_op jit(solution)/shard_map/ppermute | solution.py:25
  48.3 6.4 %copy-start.5 = (f32[2048]{0:T(1024)}, f32[2048]{0:T(1024)S(1)}, u32[]{:S(2)}) copy-start(f32[2048]{0:T(1024)S(1)} %get-tuple-element.56) | copy-start | bytes 24580
  54.7 1.2 collective-permute-start.13
  56.0 4.7 %collective-permute-start.14 = (f32[1,2304]{1,0:T(1,128)S(1)}, f32[1,2304]{1,0:T(1,128)S(1)}, u32[]{:S(2)}, u32[]{:S(2)}) collective-permute-start(f32[1,2304]{1,0:T(1,128)S(1)} %add.103), channel_id=1, source_target_pairs={{0,2},{1,3},{2,0},{3,1},{4,6},{5,7},{6,4},{7,5},{8,10},{9,11},{10,... | collective-permute-start | bytes 27656 | tf_op jit(solution)/shard_map/ppermute | solution.py:25
  56.0 5.1 %collective-permute-start.15 = (f32[1,2304]{1,0:T(1,128)S(1)}, f32[1,2304]{1,0:T(1,128)S(1)}, u32[]{:S(2)}, u32[]{:S(2)}) collective-permute-start(f32[1,2304]{1,0:T(1,128)S(1)} %add.103), channel_id=1, source_target_pairs={{0,4},{1,5},{2,6},{3,7},{4,0},{5,1},{6,2},{7,3},{8,12},{9,13},{10,... | collective-permute-start | bytes 27656 | tf_op jit(solution)/shard_map/ppermute | solution.py:25
  59.2 5.5 %collective-permute-start.16 = (f32[1,2304]{1,0:T(1,128)S(1)}, f32[1,2304]{1,0:T(1,128)S(1)}, u32[]{:S(2)}, u32[]{:S(2)}) collective-permute-start(f32[1,2304]{1,0:T(1,128)S(1)} %add.103), channel_id=1, source_target_pairs={{0,6},{1,7},{2,4},{3,5},{4,2},{5,3},{6,0},{7,1},{8,14},{9,15},{10,... | collective-permute-start | bytes 27656 | tf_op jit(solution)/shard_map/ppermute | solution.py:25
  60.6 14.1 %collective-permute-start.12 = (bf16[256,1024]{1,0:T(8,128)(2,1)S(1)}, bf16[256,1024]{1,0:T(8,128)(2,1)S(1)}, u32[]{:S(2)}, u32[]{:S(2)}) collective-permute-start(bf16[256,1024]{1,0:T(8,128)(2,1)S(1)} %get-tuple-element.62), channel_id=1, source_target_pairs={{0,24},{8,16},{16,8},{24,0},{1,25},{9,17},{17,9},{25,1},{2,26},{10... | collective-permute-start | bytes 1572872 | tf_op jit(solution)/shard_map/ppermute | solution.py:25
  81.5 71.0 %collective-permute-start.24 = (bf16[2,2,256,512]{3,2,1,0:T(8,128)(2,1)}, bf16[2,2,256,512]{3,2,1,0:T(8,128)(2,1)S(1)}, u32[]{:S(2)}, u32[]{:S(2)}) collective-permute-start(bf16[2,2,256,512]{3,2,1,0:T(8,128)(2,1)} %get-tuple-element.48), channel_id=1, source_target_pairs={{0,8},{8,0},{16,24},{24,16},{1,9},{9,1},{17,25},{25,17},{2,10},{10... | collective-permute-start | bytes 3145736 | tf_op jit(solution)/shard_map/ppermute | solution.py:25
  96.4 59.7 %collective-permute-start.20 = (bf16[2,2,256,640]{3,2,1,0:T(8,128)(2,1)}, bf16[2,2,256,640]{3,2,1,0:T(8,128)(2,1)S(1)}, u32[]{:S(2)}, u32[]{:S(2)}) collective-permute-start(bf16[2,2,256,640]{3,2,1,0:T(8,128)(2,1)} %get-tuple-element.44), channel_id=1, source_target_pairs={{0,8},{8,0},{16,24},{24,16},{1,9},{9,1},{17,25},{25,17},{2,10},{10... | collective-permute-start | bytes 3932168 | tf_op jit(solution)/shard_map/ppermute | solution.py:25
  97.9 7.6 %copy-start.13 = (f32[1024]{0:T(1024)S(1)}, f32[1024]{0:T(1024)}, u32[]{:S(2)}) copy-start(f32[1024]{0:T(1024)} %param.17) | copy-start | bytes 12292
  97.9 8.3 %copy-start.14 = (bf16[2,2,256,384]{3,2,1,0:T(8,128)(2,1)S(1)}, bf16[2,2,256,384]{3,2,1,0:T(8,128)(2,1)}, u32[]{:S(2)}) copy-start(bf16[2,2,256,384]{3,2,1,0:T(8,128)(2,1)} %get-tuple-element.50) | copy-start | bytes 2359300
  97.9 53.8 %copy-start.4 = (bf16[2,2,256,384]{3,2,1,0:T(8,128)(2,1)S(1)}, bf16[2,2,256,384]{3,2,1,0:T(8,128)(2,1)}, u32[]{:S(2)}) copy-start(bf16[2,2,256,384]{3,2,1,0:T(8,128)(2,1)} %get-tuple-element.49.refs_0_.refs_3_) | copy-start | bytes 2359300
  97.9 54.5 %copy-start.3 = (bf16[2,2,256,512]{3,2,1,0:T(8,128)(2,1)S(1)}, bf16[2,2,256,512]{3,2,1,0:T(8,128)(2,1)}, u32[]{:S(2)}) copy-start(bf16[2,2,256,512]{3,2,1,0:T(8,128)(2,1)} %get-tuple-element.47.refs_0_) | copy-start | bytes 3145732
  97.9 58.2 %copy-start = (bf16[2,2,256,640]{3,2,1,0:T(8,128)(2,1)S(1)}, bf16[2,2,256,640]{3,2,1,0:T(8,128)(2,1)}, u32[]{:S(2)}) copy-start(bf16[2,2,256,640]{3,2,1,0:T(8,128)(2,1)} %get-tuple-element.43.refs_0_) | copy-start | bytes 3932164
  105.0 48.2 %collective-permute-start.22 = (bf16[2,2,256,512]{3,2,1,0:T(8,128)(2,1)}, bf16[2,2,256,512]{3,2,1,0:T(8,128)(2,1)S(1)}, u32[]{:S(2)}, u32[]{:S(2)}) collective-permute-start(bf16[2,2,256,512]{3,2,1,0:T(8,128)(2,1)} %get-tuple-element.46), channel_id=1, source_target_pairs={{0,16},{8,24},{16,0},{24,8},{1,17},{9,25},{17,1},{25,9},{2,18},{10... | collective-permute-start | bytes 3145736 | tf_op jit(solution)/shard_map/ppermute | solution.py:25
  106.2 63.5 %copy-start.10 = (f32[1024]{0:T(1024)}, f32[1024]{0:T(1024)S(1)}, u32[]{:S(2)}) copy-start(f32[1024]{0:T(1024)S(1)} %get-tuple-element.58) | copy-start | bytes 12292
  106.2 45.4 %collective-permute-start.26 = (bf16[2,2,256,384]{3,2,1,0:T(8,128)(2,1)S(1)}, bf16[2,2,256,384]{3,2,1,0:T(8,128)(2,1)S(1)}, u32[]{:S(2)}, u32[]{:S(2)}) collective-permute-start(bf16[2,2,256,384]{3,2,1,0:T(8,128)(2,1)S(1)} %copy-done.14), channel_id=1, source_target_pairs={{0,16},{8,24},{16,0},{24,8},{1,17},{9,25},{17,1},{25,9},{2,18},{10... | collective-permute-start | bytes 2359304 | tf_op jit(solution)/shard_map/ppermute | solution.py:25
  109.7 23.6 %collective-permute-start.17 = (f32[2,128]{1,0:T(2,128)S(1)}, f32[2,128]{1,0:T(2,128)S(1)}, u32[]{:S(2)}, u32[]{:S(2)}) collective-permute-start(f32[2,128]{1,0:T(2,128)S(1)} %broadcast_in_dim.31), channel_id=1, source_target_pairs={{0,8},{8,0},{16,24},{24,16},{1,9},{9,1},{17,25},{25,17},{2,10},{10... | collective-permute-start | bytes 3080 | tf_op jit(solution)/shard_map/ppermute | solution.py:25
  133.4 11.7 %collective-permute-start.18 = (f32[2,128]{1,0:T(2,128)S(1)}, f32[2,128]{1,0:T(2,128)S(1)}, u32[]{:S(2)}, u32[]{:S(2)}) collective-permute-start(f32[2,128]{1,0:T(2,128)S(1)} %broadcast_in_dim.31), channel_id=1, source_target_pairs={{0,16},{8,24},{16,0},{24,8},{1,17},{9,25},{17,1},{25,9},{2,18},{10... | collective-permute-start | bytes 3080 | tf_op jit(solution)/shard_map/ppermute | solution.py:25
  145.1 4.5 %collective-permute-start.19 = (f32[2,128]{1,0:T(2,128)S(1)}, f32[2,128]{1,0:T(2,128)S(1)}, u32[]{:S(2)}, u32[]{:S(2)}) collective-permute-start(f32[2,128]{1,0:T(2,128)S(1)} %broadcast_in_dim.31), channel_id=1, source_target_pairs={{0,24},{8,16},{16,8},{24,0},{1,25},{9,17},{17,9},{25,1},{2,26},{10... | collective-permute-start | bytes 3080 | tf_op jit(solution)/shard_map/ppermute | solution.py:25
  151.8 17.9 %collective-permute-start.27 = (bf16[2,1,256,384]{3,2,1,0:T(8,128)(2,1)S(1)}, bf16[2,1,256,384]{3,2,1,0:T(8,128)(2,1)S(1)}, u32[]{:S(2)}, u32[]{:S(2)}) collective-permute-start(bf16[2,1,256,384]{3,2,1,0:T(8,128)(2,1)S(1)} %combine.7), channel_id=1, source_target_pairs={{0,8},{8,0},{16,24},{24,16},{1,9},{9,1},{17,25},{25,17},{2,10},{10... | collective-permute-start | bytes 1179656 | tf_op jit(solution)/shard_map/ppermute | solution.py:25
  152.6 17.1 %collective-permute-start.25 = (bf16[2,1,256,512]{3,2,1,0:T(8,128)(2,1)S(1)}, bf16[2,1,256,512]{3,2,1,0:T(8,128)(2,1)S(1)}, u32[]{:S(2)}, u32[]{:S(2)}) collective-permute-start(bf16[2,1,256,512]{3,2,1,0:T(8,128)(2,1)S(1)} %combine.6), channel_id=1, source_target_pairs={{0,16},{8,24},{16,0},{24,8},{1,17},{9,25},{17,1},{25,9},{2,18},{10... | collective-permute-start | bytes 1572872 | tf_op jit(solution)/shard_map/ppermute | solution.py:25
  153.2 1.2 copy-start.1
  154.6 16.8 %collective-permute-start.23 = (bf16[2,1,256,512]{3,2,1,0:T(8,128)(2,1)S(1)}, bf16[2,1,256,512]{3,2,1,0:T(8,128)(2,1)S(1)}, u32[]{:S(2)}, u32[]{:S(2)}) collective-permute-start(bf16[2,1,256,512]{3,2,1,0:T(8,128)(2,1)S(1)} %combine.5), channel_id=1, source_target_pairs={{0,8},{8,0},{16,24},{24,16},{1,9},{9,1},{17,25},{25,17},{2,10},{10... | collective-permute-start | bytes 1572872 | tf_op jit(solution)/shard_map/ppermute | solution.py:25
  156.3 19.8 %collective-permute-start.21 = (bf16[2,1,256,640]{3,2,1,0:T(8,128)(2,1)S(1)}, bf16[2,1,256,640]{3,2,1,0:T(8,128)(2,1)S(1)}, u32[]{:S(2)}, u32[]{:S(2)}) collective-permute-start(bf16[2,1,256,640]{3,2,1,0:T(8,128)(2,1)S(1)} %combine.4), channel_id=1, source_target_pairs={{0,16},{8,24},{16,0},{24,8},{1,17},{9,25},{17,1},{25,9},{2,18},{10... | collective-permute-start | bytes 1966088 | tf_op jit(solution)/shard_map/ppermute | solution.py:25
  157.9 18.2 %copy-start.2 = (bf16[2,2,256,512]{3,2,1,0:T(8,128)(2,1)S(1)}, bf16[2,2,256,512]{3,2,1,0:T(8,128)(2,1)}, u32[]{:S(2)}) copy-start(bf16[2,2,256,512]{3,2,1,0:T(8,128)(2,1)} %get-tuple-element.45.refs_0_.refs_3_) | copy-start | bytes 3145732
